TPU v7x, 32 devices: a whole 2x2x4 slice. The times are simulated.
32 devices in a mesh: field: 2 (over y), sky: 4 (over z), epoch: 2 (over x), vel: 2 (over core).
Axes of the slice: x: 2, y: 2, z: 4, core: 2. Of those that a mesh axis runs over, the one named last changes fastest.
Arguments:
- images: bfloat16 [64, 8, 128, 128], P(('epoch', 'vel'), ('field', 'sky')), parts along dimension 1, may hold values from -6 to 6
- variances: bfloat16 [64, 8, 128, 128], P(('epoch', 'vel'), ('field', 'sky')), parts along dimension 1, may hold values from 0.5 to 2
- valid: int32 [64, 8], P(('epoch', 'vel'), ('field', 'sky')), parts along dimension 1, may hold values from 0 to 1, as said below
- psf_sigma: float32 [128], P(('field', 'epoch', 'vel')), parts along dimension 0, may hold values from 0.8 to 2.5
- offsets: int32 [2, 16, 64], P(None, None, 'epoch'), may hold values from -12 to 12, as said below
Outputs:
- likelihood: float32 [16, 8, 128, 128], P(('epoch', 'vel'), ('field', 'sky')), parts along dimension 1
- flux: float32 [16, 8, 128, 128], P(('epoch', 'vel'), ('field', 'sky')), parts along dimension 1
There are 2 independent parts, one for each index of `field`. A program takes and returns all parts, laid end to end along the dimension named above; an argument that names none is the same for every part. Nothing has to cross between parts.
Inputs may be any that keep to these rules, and one draw needn't show every extreme that they name: Each hypothesis moves linearly: offsets[c, k, e] = floor(s[c, k] * e / 63) for integer speeds s within the range; both ends of the range are reached. `valid`: in one tile of the field, drawn from the seed, exactly one epoch is usable; in every other tile each frame is usable with probability 3/4, independently.
All inputs are finite; a program needn't handle non-finite values.
Results may differ from a plain program's by a relative error of at most 0.0058.
Values may be sent and summed in bfloat16 or wider, within the bound.
A program may use at most 64 MiB of HBM per device.

v0:
```python
import jax
import jax.numpy as jnp
from jax import lax
from jax.sharding import PartitionSpec as P

VELS = 16
REACH = 12
PSFR = 7
GRID_X = 4


phi_floor = 0.25


def shifted(block, axis, distance):
    devices = range(lax.axis_size(axis))
    route = [((i - distance) % len(devices), i) for i in devices]
    return lax.ppermute(block, axis, route)


def banded_matrix(kernel_taps, size_in, size_out):
    in_index = lax.broadcasted_iota(jnp.int32, (size_in, size_out), 0)
    out_index = lax.broadcasted_iota(jnp.int32, (size_in, size_out), 1)
    distance = in_index - out_index
    summed = jnp.zeros(kernel_taps.shape[:2] + (size_in, size_out), jnp.float32)
    for tap_index in range(kernel_taps.shape[2]):
        summed = summed + jnp.where(
            distance == tap_index, kernel_taps[:, :, tap_index, None, None], 0.0
        )
    return summed.astype(jnp.bfloat16)


def stack_block(corrected, motion, chosen):
    indices = jnp.arange(motion.shape[1], dtype=jnp.int32)
    select = (chosen[:, None] == indices[None, :]).astype(jnp.int32)
    drift_y = jnp.sum(select[:, :, None] * motion[0][None], axis=1)
    drift_x = jnp.sum(select[:, :, None] * motion[1][None], axis=1)
    tile_size = corrected.shape[-1] - 2 * REACH

    def accumulate(epoch_id, summed):
        epoch_map = lax.dynamic_index_in_dim(corrected, epoch_id, 0, keepdims=False)
        shifts_y = lax.dynamic_index_in_dim(drift_y, epoch_id, 1, keepdims=False)
        shifts_x = lax.dynamic_index_in_dim(drift_x, epoch_id, 1, keepdims=False)

        def window(shift_y, shift_x):
            start_y = REACH + shift_y
            start_x = REACH + shift_x
            return lax.dynamic_slice(
                epoch_map, (jnp.zeros((), jnp.int32), start_y, start_x), (2, tile_size, tile_size)
            )

        return summed + jax.vmap(window)(shifts_y, shifts_x)

    initial = jnp.zeros((chosen.shape[0], 2, tile_size, tile_size), jnp.float32)
    return lax.fori_loop(0, corrected.shape[0], accumulate, initial)


def on_device(images, variances, valid, psf_sigma, offsets):
    margin = REACH + PSFR
    tile_size = images.shape[-1]
    usable = valid[:, 0].astype(jnp.float32)[:, None, None]
    scaled = images[:, 0].astype(jnp.float32) / variances[:, 0].astype(jnp.float32) * usable
    inverse = usable / variances[:, 0].astype(jnp.float32)
    inputs_pair = jnp.stack([scaled.astype(jnp.bfloat16), inverse.astype(jnp.bfloat16)], axis=1)
    tile_count = lax.axis_size("sky")
    position = (lax.axis_index("sky") + GRID_X // 2) % tile_count
    column = position % GRID_X
    sides = []
    for direction in (-1, 1):
        border = (
            inputs_pair[..., tile_size - margin :] if direction == 1 else inputs_pair[..., :margin]
        )
        sides.append(shifted(border, "sky", direction))
    left_side = jnp.where(column > 0, sides[1], jnp.zeros_like(sides[1]))
    right_side = jnp.where(column < GRID_X - 1, sides[0], jnp.zeros_like(sides[0]))
    widened = jnp.concatenate([left_side, inputs_pair, right_side], axis=3)
    levels = []
    for direction in (GRID_X, -GRID_X):
        border = (
            widened[:, :, tile_size - margin :, :] if direction > 0 else widened[:, :, :margin, :]
        )
        levels.append(shifted(border, "sky", direction))
    upper = jnp.where(position >= GRID_X, levels[0], jnp.zeros_like(levels[0]))
    lower = jnp.where(position < tile_count - GRID_X, levels[1], jnp.zeros_like(levels[1]))
    extended = jnp.concatenate([upper, widened, lower], axis=2)
    spread = jnp.arange(-PSFR, PSFR + 1).astype(jnp.float32)
    profile = jnp.exp(-0.5 * (spread[None, :] / psf_sigma[:, None]) ** 2)
    profile = profile / jnp.sum(profile, axis=1, keepdims=True)
    kernel_taps = jnp.stack(
        [profile.astype(jnp.bfloat16), (profile * profile).astype(jnp.bfloat16)], axis=1
    ).astype(jnp.float32)
    size_in = tile_size + 2 * margin
    size_out = tile_size + 2 * REACH
    banded = banded_matrix(kernel_taps, size_in, size_out)
    rows_done = jnp.einsum(
        "emio,emix->emox", banded, extended, preferred_element_type=jnp.float32
    ).astype(jnp.bfloat16)
    corrected = jnp.einsum("emox,emxp->emop", rows_done, banded, preferred_element_type=jnp.float32)
    pairs = lax.axis_size("vel")
    member = lax.axis_index("vel")
    block = VELS // (lax.axis_size("epoch") * pairs)
    shared = lax.all_gather(corrected, "vel", axis=0, tiled=True)
    row_ids = jnp.arange(lax.axis_size("epoch") * block, dtype=jnp.int32)
    chosen = (row_ids // block * pairs + member) * block + row_ids % block
    sums = lax.psum_scatter(
        stack_block(shared, offsets, chosen), "epoch", scatter_dimension=0, tiled=True
    )
    psi_sum = sums[:, 0]
    phi_sum = jnp.maximum(sums[:, 1], phi_floor)
    likelihood = psi_sum / jnp.sqrt(phi_sum)
    flux = psi_sum / phi_sum
    return (likelihood[:, None], flux[:, None])


def solution(mesh):
    placed = (
        P(("epoch", "vel"), ("field", "sky"), None, None),
        P(("epoch", "vel"), ("field", "sky"), None, None),
        P(("epoch", "vel"), ("field", "sky")),
        P(("field", "epoch", "vel")),
        P(None, None, "epoch"),
    )
    return jax.shard_map(
        on_device,
        mesh=mesh,
        in_specs=placed,
        out_specs=(
            P(("epoch", "vel"), ("field", "sky"), None, None),
            P(("epoch", "vel"), ("field", "sky"), None, None),
        ),
        check_vma=False,
    )
```

profile of v0, /device:TPU:0, one launch (start us, length us, event | category | flops | bytes accessed | tf_op | source)
XLA Modules:
  0.0 636.6 jit_solution(12161071059608015529)
XLA Ops:
  7.9 1.6 fusion.19
  10.4 3.1 collective-permute-start
  13.9 2.1 collective-permute-start.1
  33.6 20.2 %fusion.12 = f32[16,2,152,152]{3,2,1,0:T(8,128)} fusion(bf16[16,2,19,166]{3,2,1,0:T(8,128)(2,1)S(1)} %copy_select_fusion, bf16[16,2,128,19]{3,2,1,0:T(8,128)(2,1)S(1)} %copy.113, bf16[16,1,128,128]{3,2,1,0:T(8,128)(2,1)S(1)} %get-tuple-element.217, bf16[16,1,128,128]{3,2,1,0:T(8,128)(2,1)S(1)} %get-tuple-element.216, ...), kind=kOutput, calls=%fused_computation.22 | convolution fusion | flops 573356032 | bytes 5101296 | tf_op jit(solution)/shard_map/emox,emxp->emop/dot_general | solution.py:98
  54.7 21.0 %all-gather.2.cloned.1.call-done = f32[32,2,152,152]{3,2,1,0:T(8,128)} async-done(((f32[16,2,152,152]{3,2,1,0:T(8,128)}), f32[32,2,152,152]{3,2,1,0:T(8,128)}) %all-gather.2.cloned.1.call-update) | async-done | bytes 5914640 | tf_op jit(solution)/shard_map/all_gather | solution.py:102
  75.8 529.3 %while.24 = (s32[]{:T(128)}, f32[8,2,128,128]{3,2,1,0:T(8,128)S(1)}, f32[32,2,152,152]{3,2,1,0:T(8,128)}, s32[8,32]{0,1:T(8,128)S(1)}, s32[8,32]{0,1:T(8,128)S(1)}, /*index=5*/s32[]{:T(128)}, s32[]{:T(128)}, f32[]{:T(128)}) while((s32[]{:T(128)}, f32[8,2,128,128]{3,2,1,0:T(8,128)S(1)}, f32[32,2,152,152]{3,2,1,0:T(8,128)}, ...), condition=%wide.region_4.5_spmd.clone.clone, body=%wide.region_3.4_spmd.clone.sunk.clone | while | flops 524405 | bytes 3778160 | solution.py:55
  76.8 15.1 %while.23 = (s32[]{:T(128)}, f32[2,152,152]{2,1,0:T(8,128)S(1)}, s32[8,3]{0,1:T(4,128)S(1)}, f32[8,2,128,128]{3,2,1,0:T(8,128)S(1)}, s32[]{:T(128)}) while((s32[]{:T(128)}, f32[2,152,152]{2,1,0:T(8,128)S(1)}, s32[8,3]{0,1:T(4,128)S(1)}, f32[8,2,128,128]{3,2,1,0:T(8,128)S(1)}, s32[]{:T(128)}) %tuple.104), condition=%wide.while_cond, body=%wide.while_body.sunk | while | flops 2 | bytes 262261 | solution.py:48
  81.2 1.3 bitcast_dynamic-update-slice_fusion.2
  83.1 1.3 bitcast_dynamic-update-slice_fusion.2
  85.0 1.3 bitcast_dynamic-update-slice_fusion.2
  86.9 1.3 bitcast_dynamic-update-slice_fusion.2
  88.8 1.3 bitcast_dynamic-update-slice_fusion.2
  90.7 1.3 bitcast_dynamic-update-slice_fusion.2
  93.4 15.1 %while.23 = (s32[]{:T(128)}, f32[2,152,152]{2,1,0:T(8,128)S(1)}, s32[8,3]{0,1:T(4,128)S(1)}, f32[8,2,128,128]{3,2,1,0:T(8,128)S(1)}, s32[]{:T(128)}) while((s32[]{:T(128)}, f32[2,152,152]{2,1,0:T(8,128)S(1)}, s32[8,3]{0,1:T(4,128)S(1)}, f32[8,2,128,128]{3,2,1,0:T(8,128)S(1)}, s32[]{:T(128)}) %tuple.104), condition=%wide.while_cond, body=%wide.while_body.sunk | while | flops 2 | bytes 262261 | solution.py:48
  94.0 1.3 bitcast_dynamic-update-slice_fusion.2
  95.9 1.3 bitcast_dynamic-update-slice_fusion.2
  109.9 15.1 %while.23 = (s32[]{:T(128)}, f32[2,152,152]{2,1,0:T(8,128)S(1)}, s32[8,3]{0,1:T(4,128)S(1)}, f32[8,2,128,128]{3,2,1,0:T(8,128)S(1)}, s32[]{:T(128)}) while((s32[]{:T(128)}, f32[2,152,152]{2,1,0:T(8,128)S(1)}, s32[8,3]{0,1:T(4,128)S(1)}, f32[8,2,128,128]{3,2,1,0:T(8,128)S(1)}, s32[]{:T(128)}) %tuple.104), condition=%wide.while_cond, body=%wide.while_body.sunk | while | flops 2 | bytes 262261 | solution.py:48
  126.4 15.1 %while.23 = (s32[]{:T(128)}, f32[2,152,152]{2,1,0:T(8,128)S(1)}, s32[8,3]{0,1:T(4,128)S(1)}, f32[8,2,128,128]{3,2,1,0:T(8,128)S(1)}, s32[]{:T(128)}) while((s32[]{:T(128)}, f32[2,152,152]{2,1,0:T(8,128)S(1)}, s32[8,3]{0,1:T(4,128)S(1)}, f32[8,2,128,128]{3,2,1,0:T(8,128)S(1)}, s32[]{:T(128)}) %tuple.104), condition=%wide.while_cond, body=%wide.while_body.sunk | while | flops 2 | bytes 262261 | solution.py:48
  143.0 15.1 %while.23 = (s32[]{:T(128)}, f32[2,152,152]{2,1,0:T(8,128)S(1)}, s32[8,3]{0,1:T(4,128)S(1)}, f32[8,2,128,128]{3,2,1,0:T(8,128)S(1)}, s32[]{:T(128)}) while((s32[]{:T(128)}, f32[2,152,152]{2,1,0:T(8,128)S(1)}, s32[8,3]{0,1:T(4,128)S(1)}, f32[8,2,128,128]{3,2,1,0:T(8,128)S(1)}, s32[]{:T(128)}) %tuple.104), condition=%wide.while_cond, body=%wide.while_body.sunk | while | flops 2 | bytes 262261 | solution.py:48
  159.5 15.1 %while.23 = (s32[]{:T(128)}, f32[2,152,152]{2,1,0:T(8,128)S(1)}, s32[8,3]{0,1:T(4,128)S(1)}, f32[8,2,128,128]{3,2,1,0:T(8,128)S(1)}, s32[]{:T(128)}) while((s32[]{:T(128)}, f32[2,152,152]{2,1,0:T(8,128)S(1)}, s32[8,3]{0,1:T(4,128)S(1)}, f32[8,2,128,128]{3,2,1,0:T(8,128)S(1)}, s32[]{:T(128)}) %tuple.104), condition=%wide.while_cond, body=%wide.while_body.sunk | while | flops 2 | bytes 262261 | solution.py:48
  176.1 15.1 %while.23 = (s32[]{:T(128)}, f32[2,152,152]{2,1,0:T(8,128)S(1)}, s32[8,3]{0,1:T(4,128)S(1)}, f32[8,2,128,128]{3,2,1,0:T(8,128)S(1)}, s32[]{:T(128)}) while((s32[]{:T(128)}, f32[2,152,152]{2,1,0:T(8,128)S(1)}, s32[8,3]{0,1:T(4,128)S(1)}, f32[8,2,128,128]{3,2,1,0:T(8,128)S(1)}, s32[]{:T(128)}) %tuple.104), condition=%wide.while_cond, body=%wide.while_body.sunk | while | flops 2 | bytes 262261 | solution.py:48
  192.6 15.1 %while.23 = (s32[]{:T(128)}, f32[2,152,152]{2,1,0:T(8,128)S(1)}, s32[8,3]{0,1:T(4,128)S(1)}, f32[8,2,128,128]{3,2,1,0:T(8,128)S(1)}, s32[]{:T(128)}) while((s32[]{:T(128)}, f32[2,152,152]{2,1,0:T(8,128)S(1)}, s32[8,3]{0,1:T(4,128)S(1)}, f32[8,2,128,128]{3,2,1,0:T(8,128)S(1)}, s32[]{:T(128)}) %tuple.104), condition=%wide.while_cond, body=%wide.while_body.sunk | while | flops 2 | bytes 262261 | solution.py:48
  209.2 15.1 %while.23 = (s32[]{:T(128)}, f32[2,152,152]{2,1,0:T(8,128)S(1)}, s32[8,3]{0,1:T(4,128)S(1)}, f32[8,2,128,128]{3,2,1,0:T(8,128)S(1)}, s32[]{:T(128)}) while((s32[]{:T(128)}, f32[2,152,152]{2,1,0:T(8,128)S(1)}, s32[8,3]{0,1:T(4,128)S(1)}, f32[8,2,128,128]{3,2,1,0:T(8,128)S(1)}, s32[]{:T(128)}) %tuple.104), condition=%wide.while_cond, body=%wide.while_body.sunk | while | flops 2 | bytes 262261 | solution.py:48
  225.7 15.1 %while.23 = (s32[]{:T(128)}, f32[2,152,152]{2,1,0:T(8,128)S(1)}, s32[8,3]{0,1:T(4,128)S(1)}, f32[8,2,128,128]{3,2,1,0:T(8,128)S(1)}, s32[]{:T(128)}) while((s32[]{:T(128)}, f32[2,152,152]{2,1,0:T(8,128)S(1)}, s32[8,3]{0,1:T(4,128)S(1)}, f32[8,2,128,128]{3,2,1,0:T(8,128)S(1)}, s32[]{:T(128)}) %tuple.104), condition=%wide.while_cond, body=%wide.while_body.sunk | while | flops 2 | bytes 262261 | solution.py:48
  242.2 15.1 %while.23 = (s32[]{:T(128)}, f32[2,152,152]{2,1,0:T(8,128)S(1)}, s32[8,3]{0,1:T(4,128)S(1)}, f32[8,2,128,128]{3,2,1,0:T(8,128)S(1)}, s32[]{:T(128)}) while((s32[]{:T(128)}, f32[2,152,152]{2,1,0:T(8,128)S(1)}, s32[8,3]{0,1:T(4,128)S(1)}, f32[8,2,128,128]{3,2,1,0:T(8,128)S(1)}, s32[]{:T(128)}) %tuple.104), condition=%wide.while_cond, body=%wide.while_body.sunk | while | flops 2 | bytes 262261 | solution.py:48
  258.8 15.1 %while.23 = (s32[]{:T(128)}, f32[2,152,152]{2,1,0:T(8,128)S(1)}, s32[8,3]{0,1:T(4,128)S(1)}, f32[8,2,128,128]{3,2,1,0:T(8,128)S(1)}, s32[]{:T(128)}) while((s32[]{:T(128)}, f32[2,152,152]{2,1,0:T(8,128)S(1)}, s32[8,3]{0,1:T(4,128)S(1)}, f32[8,2,128,128]{3,2,1,0:T(8,128)S(1)}, s32[]{:T(128)}) %tuple.104), condition=%wide.while_cond, body=%wide.while_body.sunk | while | flops 2 | bytes 262261 | solution.py:48
  275.3 15.1 %while.23 = (s32[]{:T(128)}, f32[2,152,152]{2,1,0:T(8,128)S(1)}, s32[8,3]{0,1:T(4,128)S(1)}, f32[8,2,128,128]{3,2,1,0:T(8,128)S(1)}, s32[]{:T(128)}) while((s32[]{:T(128)}, f32[2,152,152]{2,1,0:T(8,128)S(1)}, s32[8,3]{0,1:T(4,128)S(1)}, f32[8,2,128,128]{3,2,1,0:T(8,128)S(1)}, s32[]{:T(128)}) %tuple.104), condition=%wide.while_cond, body=%wide.while_body.sunk | while | flops 2 | bytes 262261 | solution.py:48
  291.9 15.1 %while.23 = (s32[]{:T(128)}, f32[2,152,152]{2,1,0:T(8,128)S(1)}, s32[8,3]{0,1:T(4,128)S(1)}, f32[8,2,128,128]{3,2,1,0:T(8,128)S(1)}, s32[]{:T(128)}) while((s32[]{:T(128)}, f32[2,152,152]{2,1,0:T(8,128)S(1)}, s32[8,3]{0,1:T(4,128)S(1)}, f32[8,2,128,128]{3,2,1,0:T(8,128)S(1)}, s32[]{:T(128)}) %tuple.104), condition=%wide.while_cond, body=%wide.while_body.sunk | while | flops 2 | bytes 262261 | solution.py:48
  308.4 15.1 %while.23 = (s32[]{:T(128)}, f32[2,152,152]{2,1,0:T(8,128)S(1)}, s32[8,3]{0,1:T(4,128)S(1)}, f32[8,2,128,128]{3,2,1,0:T(8,128)S(1)}, s32[]{:T(128)}) while((s32[]{:T(128)}, f32[2,152,152]{2,1,0:T(8,128)S(1)}, s32[8,3]{0,1:T(4,128)S(1)}, f32[8,2,128,128]{3,2,1,0:T(8,128)S(1)}, s32[]{:T(128)}) %tuple.104), condition=%wide.while_cond, body=%wide.while_body.sunk | while | flops 2 | bytes 262261 | solution.py:48
  325.0 15.1 %while.23 = (s32[]{:T(128)}, f32[2,152,152]{2,1,0:T(8,128)S(1)}, s32[8,3]{0,1:T(4,128)S(1)}, f32[8,2,128,128]{3,2,1,0:T(8,128)S(1)}, s32[]{:T(128)}) while((s32[]{:T(128)}, f32[2,152,152]{2,1,0:T(8,128)S(1)}, s32[8,3]{0,1:T(4,128)S(1)}, f32[8,2,128,128]{3,2,1,0:T(8,128)S(1)}, s32[]{:T(128)}) %tuple.104), condition=%wide.while_cond, body=%wide.while_body.sunk | while | flops 2 | bytes 262261 | solution.py:48
  341.5 15.1 %while.23 = (s32[]{:T(128)}, f32[2,152,152]{2,1,0:T(8,128)S(1)}, s32[8,3]{0,1:T(4,128)S(1)}, f32[8,2,128,128]{3,2,1,0:T(8,128)S(1)}, s32[]{:T(128)}) while((s32[]{:T(128)}, f32[2,152,152]{2,1,0:T(8,128)S(1)}, s32[8,3]{0,1:T(4,128)S(1)}, f32[8,2,128,128]{3,2,1,0:T(8,128)S(1)}, s32[]{:T(128)}) %tuple.104), condition=%wide.while_cond, body=%wide.while_body.sunk | while | flops 2 | bytes 262261 | solution.py:48
  358.0 15.1 %while.23 = (s32[]{:T(128)}, f32[2,152,152]{2,1,0:T(8,128)S(1)}, s32[8,3]{0,1:T(4,128)S(1)}, f32[8,2,128,128]{3,2,1,0:T(8,128)S(1)}, s32[]{:T(128)}) while((s32[]{:T(128)}, f32[2,152,152]{2,1,0:T(8,128)S(1)}, s32[8,3]{0,1:T(4,128)S(1)}, f32[8,2,128,128]{3,2,1,0:T(8,128)S(1)}, s32[]{:T(128)}) %tuple.104), condition=%wide.while_cond, body=%wide.while_body.sunk | while | flops 2 | bytes 262261 | solution.py:48
  374.6 15.1 %while.23 = (s32[]{:T(128)}, f32[2,152,152]{2,1,0:T(8,128)S(1)}, s32[8,3]{0,1:T(4,128)S(1)}, f32[8,2,128,128]{3,2,1,0:T(8,128)S(1)}, s32[]{:T(128)}) while((s32[]{:T(128)}, f32[2,152,152]{2,1,0:T(8,128)S(1)}, s32[8,3]{0,1:T(4,128)S(1)}, f32[8,2,128,128]{3,2,1,0:T(8,128)S(1)}, s32[]{:T(128)}) %tuple.104), condition=%wide.while_cond, body=%wide.while_body.sunk | while | flops 2 | bytes 262261 | solution.py:48
  391.1 15.1 %while.23 = (s32[]{:T(128)}, f32[2,152,152]{2,1,0:T(8,128)S(1)}, s32[8,3]{0,1:T(4,128)S(1)}, f32[8,2,128,128]{3,2,1,0:T(8,128)S(1)}, s32[]{:T(128)}) while((s32[]{:T(128)}, f32[2,152,152]{2,1,0:T(8,128)S(1)}, s32[8,3]{0,1:T(4,128)S(1)}, f32[8,2,128,128]{3,2,1,0:T(8,128)S(1)}, s32[]{:T(128)}) %tuple.104), condition=%wide.while_cond, body=%wide.while_body.sunk | while | flops 2 | bytes 262261 | solution.py:48
  407.7 15.1 %while.23 = (s32[]{:T(128)}, f32[2,152,152]{2,1,0:T(8,128)S(1)}, s32[8,3]{0,1:T(4,128)S(1)}, f32[8,2,128,128]{3,2,1,0:T(8,128)S(1)}, s32[]{:T(128)}) while((s32[]{:T(128)}, f32[2,152,152]{2,1,0:T(8,128)S(1)}, s32[8,3]{0,1:T(4,128)S(1)}, f32[8,2,128,128]{3,2,1,0:T(8,128)S(1)}, s32[]{:T(128)}) %tuple.104), condition=%wide.while_cond, body=%wide.while_body.sunk | while | flops 2 | bytes 262261 | solution.py:48
  424.2 15.1 %while.23 = (s32[]{:T(128)}, f32[2,152,152]{2,1,0:T(8,128)S(1)}, s32[8,3]{0,1:T(4,128)S(1)}, f32[8,2,128,128]{3,2,1,0:T(8,128)S(1)}, s32[]{:T(128)}) while((s32[]{:T(128)}, f32[2,152,152]{2,1,0:T(8,128)S(1)}, s32[8,3]{0,1:T(4,128)S(1)}, f32[8,2,128,128]{3,2,1,0:T(8,128)S(1)}, s32[]{:T(128)}) %tuple.104), condition=%wide.while_cond, body=%wide.while_body.sunk | while | flops 2 | bytes 262261 | solution.py:48
  440.8 15.1 %while.23 = (s32[]{:T(128)}, f32[2,152,152]{2,1,0:T(8,128)S(1)}, s32[8,3]{0,1:T(4,128)S(1)}, f32[8,2,128,128]{3,2,1,0:T(8,128)S(1)}, s32[]{:T(128)}) while((s32[]{:T(128)}, f32[2,152,152]{2,1,0:T(8,128)S(1)}, s32[8,3]{0,1:T(4,128)S(1)}, f32[8,2,128,128]{3,2,1,0:T(8,128)S(1)}, s32[]{:T(128)}) %tuple.104), condition=%wide.while_cond, body=%wide.while_body.sunk | while | flops 2 | bytes 262261 | solution.py:48
  457.3 15.1 %while.23 = (s32[]{:T(128)}, f32[2,152,152]{2,1,0:T(8,128)S(1)}, s32[8,3]{0,1:T(4,128)S(1)}, f32[8,2,128,128]{3,2,1,0:T(8,128)S(1)}, s32[]{:T(128)}) while((s32[]{:T(128)}, f32[2,152,152]{2,1,0:T(8,128)S(1)}, s32[8,3]{0,1:T(4,128)S(1)}, f32[8,2,128,128]{3,2,1,0:T(8,128)S(1)}, s32[]{:T(128)}) %tuple.104), condition=%wide.while_cond, body=%wide.while_body.sunk | while | flops 2 | bytes 262261 | solution.py:48
  473.8 15.1 %while.23 = (s32[]{:T(128)}, f32[2,152,152]{2,1,0:T(8,128)S(1)}, s32[8,3]{0,1:T(4,128)S(1)}, f32[8,2,128,128]{3,2,1,0:T(8,128)S(1)}, s32[]{:T(128)}) while((s32[]{:T(128)}, f32[2,152,152]{2,1,0:T(8,128)S(1)}, s32[8,3]{0,1:T(4,128)S(1)}, f32[8,2,128,128]{3,2,1,0:T(8,128)S(1)}, s32[]{:T(128)}) %tuple.104), condition=%wide.while_cond, body=%wide.while_body.sunk | while | flops 2 | bytes 262261 | solution.py:48
  490.4 15.1 %while.23 = (s32[]{:T(128)}, f32[2,152,152]{2,1,0:T(8,128)S(1)}, s32[8,3]{0,1:T(4,128)S(1)}, f32[8,2,128,128]{3,2,1,0:T(8,128)S(1)}, s32[]{:T(128)}) while((s32[]{:T(128)}, f32[2,152,152]{2,1,0:T(8,128)S(1)}, s32[8,3]{0,1:T(4,128)S(1)}, f32[8,2,128,128]{3,2,1,0:T(8,128)S(1)}, s32[]{:T(128)}) %tuple.104), condition=%wide.while_cond, body=%wide.while_body.sunk | while | flops 2 | bytes 262261 | solution.py:48
  506.9 15.1 %while.23 = (s32[]{:T(128)}, f32[2,152,152]{2,1,0:T(8,128)S(1)}, s32[8,3]{0,1:T(4,128)S(1)}, f32[8,2,128,128]{3,2,1,0:T(8,128)S(1)}, s32[]{:T(128)}) while((s32[]{:T(128)}, f32[2,152,152]{2,1,0:T(8,128)S(1)}, s32[8,3]{0,1:T(4,128)S(1)}, f32[8,2,128,128]{3,2,1,0:T(8,128)S(1)}, s32[]{:T(128)}) %tuple.104), condition=%wide.while_cond, body=%wide.while_body.sunk | while | flops 2 | bytes 262261 | solution.py:48
  523.5 15.1 %while.23 = (s32[]{:T(128)}, f32[2,152,152]{2,1,0:T(8,128)S(1)}, s32[8,3]{0,1:T(4,128)S(1)}, f32[8,2,128,128]{3,2,1,0:T(8,128)S(1)}, s32[]{:T(128)}) while((s32[]{:T(128)}, f32[2,152,152]{2,1,0:T(8,128)S(1)}, s32[8,3]{0,1:T(4,128)S(1)}, f32[8,2,128,128]{3,2,1,0:T(8,128)S(1)}, s32[]{:T(128)}) %tuple.104), condition=%wide.while_cond, body=%wide.while_body.sunk | while | flops 2 | bytes 262261 | solution.py:48
  540.0 15.1 %while.23 = (s32[]{:T(128)}, f32[2,152,152]{2,1,0:T(8,128)S(1)}, s32[8,3]{0,1:T(4,128)S(1)}, f32[8,2,128,128]{3,2,1,0:T(8,128)S(1)}, s32[]{:T(128)}) while((s32[]{:T(128)}, f32[2,152,152]{2,1,0:T(8,128)S(1)}, s32[8,3]{0,1:T(4,128)S(1)}, f32[8,2,128,128]{3,2,1,0:T(8,128)S(1)}, s32[]{:T(128)}) %tuple.104), condition=%wide.while_cond, body=%wide.while_body.sunk | while | flops 2 | bytes 262261 | solution.py:48
  556.6 15.1 %while.23 = (s32[]{:T(128)}, f32[2,152,152]{2,1,0:T(8,128)S(1)}, s32[8,3]{0,1:T(4,128)S(1)}, f32[8,2,128,128]{3,2,1,0:T(8,128)S(1)}, s32[]{:T(128)}) while((s32[]{:T(128)}, f32[2,152,152]{2,1,0:T(8,128)S(1)}, s32[8,3]{0,1:T(4,128)S(1)}, f32[8,2,128,128]{3,2,1,0:T(8,128)S(1)}, s32[]{:T(128)}) %tuple.104), condition=%wide.while_cond, body=%wide.while_body.sunk | while | flops 2 | bytes 262261 | solution.py:48
  573.1 15.1 %while.23 = (s32[]{:T(128)}, f32[2,152,152]{2,1,0:T(8,128)S(1)}, s32[8,3]{0,1:T(4,128)S(1)}, f32[8,2,128,128]{3,2,1,0:T(8,128)S(1)}, s32[]{:T(128)}) while((s32[]{:T(128)}, f32[2,152,152]{2,1,0:T(8,128)S(1)}, s32[8,3]{0,1:T(4,128)S(1)}, f32[8,2,128,128]{3,2,1,0:T(8,128)S(1)}, s32[]{:T(128)}) %tuple.104), condition=%wide.while_cond, body=%wide.while_body.sunk | while | flops 2 | bytes 262261 | solution.py:48
  589.6 15.1 %while.23 = (s32[]{:T(128)}, f32[2,152,152]{2,1,0:T(8,128)S(1)}, s32[8,3]{0,1:T(4,128)S(1)}, f32[8,2,128,128]{3,2,1,0:T(8,128)S(1)}, s32[]{:T(128)}) while((s32[]{:T(128)}, f32[2,152,152]{2,1,0:T(8,128)S(1)}, s32[8,3]{0,1:T(4,128)S(1)}, f32[8,2,128,128]{3,2,1,0:T(8,128)S(1)}, s32[]{:T(128)}) %tuple.104), condition=%wide.while_cond, body=%wide.while_body.sunk | while | flops 2 | bytes 262261 | solution.py:48
  606.1 21.7 %reduce-scatter.2.cloned.1.call-done = f32[4,2,128,128]{3,2,1,0:T(8,128)} async-done(((f32[8,2,128,128]{3,2,1,0:T(8,128)}), f32[4,2,128,128]{3,2,1,0:T(8,128)}) %reduce-scatter.2.cloned.1.call-update) | async-done | bytes 524304 | tf_op jit(solution)/shard_map/reduce_scatter | solution.py:105
  627.9 1.9 slice_divide_fusion
  (1016 shorter events, 532.7 us)
Async XLA Ops:
  7.2 11.5 %copy-start.2 = (f32[16]{0:T(128)S(1)}, f32[16]{0:T(128)}, u32[]{:S(2)}) copy-start(f32[16]{0:T(128)} %param.10) | copy-start | bytes 196
  7.2 68.6 %all-gather.2.cloned.1.call-start = ((), (), s32[]{:S(2)}) async-start(), calls=%async_computation.1 | async-start | bytes 14942208 | tf_op jit(solution)/shard_map/all_gather | solution.py:102
  10.4 18.9 %collective-permute-start = (bf16[16,2,128,19]{2,0,3,1:T(8,128)(2,1)S(1)}, bf16[16,2,128,19]{2,0,3,1:T(8,128)(2,1)S(1)}, u32[]{:S(2)}, u32[]{:S(2)}) collective-permute-start(bf16[16,2,128,19]{2,0,3,1:T(8,128)(2,1)S(1)} %copy.110), channel_id=1, source_target_pairs={{12,0},{0,4},{4,8},{8,12},{13,1},{1,5},{5,9},{9,13},{14,2},{2,6},{... | collective-permute-start | bytes 466952 | tf_op jit(solution)/shard_map/ppermute | solution.py:18
  13.9 15.9 %collective-permute-start.1 = (bf16[16,2,128,19]{2,0,3,1:T(8,128)(2,1)S(1)}, bf16[16,2,128,19]{2,0,3,1:T(8,128)(2,1)S(1)}, u32[]{:S(2)}, u32[]{:S(2)}) collective-permute-start(bf16[16,2,128,19]{2,0,3,1:T(8,128)(2,1)S(1)} %copy.111), channel_id=1, source_target_pairs={{4,0},{8,4},{12,8},{0,12},{5,1},{9,5},{13,9},{1,13},{6,2},{10,6},{... | collective-permute-start | bytes 466952 | tf_op jit(solution)/shard_map/ppermute | solution.py:18
  31.1 1.5 collective-permute-start.3
  32.5 0.2 collective-permute-start.2
  53.8 0.7 copy-start.1
  53.8 574.1 %reduce-scatter.2.cloned.1.call-start = ((), (), s32[]{:S(2)}) async-start(), calls=%async_computation.2 | async-start | bytes 1572864 | tf_op jit(solution)/shard_map/reduce_scatter | solution.py:105
  605.1 1.0 copy-start
Sparse Core Ops, SparseCore 0:
  53.9 21.8 all-gather.1
  606.3 21.5 reduce-scatter.1
where the time goes:
time: 642 us; the launch traced here: 637 us
  local copies, waits for them, and re-layouts  522 us (81%)
  waiting for transfers between devices  42.8 us (7%)
  other arithmetic  23.9 us (4%)
  matrix products  20.2 us (3%)
  between operations  14.2 us (2%)
  loops' own time  7.93 us (1%)
    gather x768, local copies, waits for them, and re-layouts  478 us
    squeeze x32, local copies, waits for them, and re-layouts, accumulate(): epoch_map = lax.dynamic_index_in_dim(corrected, epoch_id, 0, keepdims=False)  31.8 us
    reduce_scatter x1, waiting for transfers between devices, on_device(): lax.psum_scatter(stack_block(shared, offsets, chosen), 'epoch', scatter_d...  21.7 us
    all_gather x1, waiting for transfers between devices, on_device(): shared = lax.all_gather(corrected, 'vel', axis=0, tiled=True)  21 us
    dot_general x1, matrix products, on_device(): jnp.einsum('emox,emxp->emop', rows_done, banded, preferred_element_type=j...  20.2 us
  transfers between devices with their start and end apart: 6, of which 2 were waited for; matrix products, arithmetic and copies ran while one was open for 3% of the time, Pallas kernels for 0%

commit v1 on v0

v1 whole, which is shorter than its diff:
```python
import functools

import jax
import jax.numpy as jnp
from jax import lax
from jax.experimental import pallas as pl
from jax.experimental.pallas import tpu as pltpu
from jax.sharding import PartitionSpec as P

VELS = 16
REACH = 12
PSFR = 7
GRID_X = 4
MARGIN = REACH + PSFR
LANES = 128

phi_floor = 0.25


def shifted(block, axis, distance):
    devices = range(lax.axis_size(axis))
    route = [((i - distance) % len(devices), i) for i in devices]
    return lax.ppermute(block, axis, route)


def positions(index, tile):
    return jnp.where(
        index < tile,
        index,
        jnp.where(
            index < tile + MARGIN,
            index - tile - MARGIN,
            jnp.where(index < tile + 2 * MARGIN, index - MARGIN, 4 * tile),
        ),
    )


def band(held, out, sigma, scale, tile):
    distance = positions(held, tile) - (out - REACH)
    away = distance.astype(jnp.float32) / sigma
    profile = jnp.exp(-0.5 * away * away) * scale
    profile = jnp.where(jnp.abs(distance) <= PSFR, profile, 0.0)
    return profile.astype(jnp.bfloat16), (profile * profile).astype(jnp.bfloat16)


def stack_kernel(tile, offsets, sigmas, order, first, own, halo, out, plane_a, plane_b):
    epochs, maps, rows_in, _ = own.shape
    rows_out = plane_a.shape[1]
    width = 2 * LANES

    def correlate(e, carry):
        sigma = jnp.full((8, LANES), sigmas[e], jnp.float32)
        tap = lax.broadcasted_iota(jnp.int32, (8, LANES), 1) - PSFR
        spread = tap.astype(jnp.float32) / sigma
        norm = jnp.sum(
            jnp.where(jnp.abs(tap) <= PSFR, jnp.exp(-0.5 * spread * spread), 0.0),
            axis=1,
            keepdims=True,
        )
        scale = (1.0 / norm)[:1]
        sig = sigma[:1, :1]
        shape = (rows_out, rows_in)
        row_bands = band(
            lax.broadcasted_iota(jnp.int32, shape, 1),
            lax.broadcasted_iota(jnp.int32, shape, 0),
            sig, scale, tile,
        )
        shape = (width, width)
        col_bands = band(
            lax.broadcasted_iota(jnp.int32, shape, 0),
            lax.broadcasted_iota(jnp.int32, shape, 1),
            sig, scale, tile,
        )
        for m in range(maps):
            held = jnp.concatenate([own[e, m], halo[e, m]], axis=1)
            rows = jnp.dot(row_bands[m], held, preferred_element_type=jnp.float32)
            done = jnp.dot(
                rows.astype(jnp.bfloat16), col_bands[m], preferred_element_type=jnp.float32
            )
            plane_a[maps * e + m] = done[:, :LANES]
            plane_b[maps * e + m] = done[:, LANES:]
        return carry

    lax.fori_loop(0, epochs, correlate, 0)
    lane = lax.broadcasted_iota(jnp.int32, (tile, LANES), 1)

    def stack(slot, carry):
        k = order[slot]
        summed = [jnp.zeros((tile, LANES), jnp.float32) for _ in range(maps)]
        for e in range(epochs):
            down = offsets[0, k, first[0] + e] + REACH
            right = offsets[1, k, first[0] + e] + REACH
            for m in range(maps):
                left_part = plane_a[maps * e + m, pl.ds(down, tile), :]
                right_part = plane_b[maps * e + m, pl.ds(down, tile), :]
                merged = jnp.where(lane >= right, left_part, right_part)
                summed[m] += pltpu.roll(merged, LANES - right, axis=1)
        for m in range(maps):
            out[slot, m] = summed[m].astype(jnp.bfloat16)
        return carry

    lax.fori_loop(0, out.shape[0], stack, 0)


def on_device(images, variances, valid, psf_sigma, offsets):
    epochs = images.shape[0]
    tile = images.shape[-1]
    usable = valid[:, 0].astype(jnp.float32)[:, None, None]
    scaled = images[:, 0].astype(jnp.float32) / variances[:, 0].astype(jnp.float32) * usable
    inverse = usable / variances[:, 0].astype(jnp.float32)
    own = jnp.stack([scaled.astype(jnp.bfloat16), inverse.astype(jnp.bfloat16)], axis=1)
    tile_count = lax.axis_size("sky")
    position = (lax.axis_index("sky") + GRID_X // 2) % tile_count
    column = position % GRID_X
    left = shifted(own[..., tile - MARGIN :], "sky", 1)
    right = shifted(own[..., :MARGIN], "sky", -1)
    left = jnp.where(column > 0, left, jnp.zeros_like(left))
    right = jnp.where(column < GRID_X - 1, right, jnp.zeros_like(right))
    blank = jnp.zeros(own.shape[:3] + (LANES - 2 * MARGIN,), jnp.bfloat16)
    halo = jnp.concatenate([left, right, blank], axis=3)
    if tile_count > GRID_X:
        both = jnp.concatenate([own, halo], axis=3)
        upper = shifted(both[:, :, tile - MARGIN :], "sky", GRID_X)
        lower = shifted(both[:, :, :MARGIN], "sky", -GRID_X)
        upper = jnp.where(position >= GRID_X, upper, jnp.zeros_like(upper))
        lower = jnp.where(position < tile_count - GRID_X, lower, jnp.zeros_like(lower))
        blank = jnp.zeros(both.shape[:2] + (LANES - 2 * MARGIN, both.shape[3]), jnp.bfloat16)
        both = jnp.concatenate([both, upper, lower, blank], axis=2)
        own, halo = both[..., :tile], both[..., tile:]
    pairs = lax.axis_size("vel")
    blocks = lax.axis_size("epoch")
    member = lax.axis_index("vel")
    group = lax.axis_index("epoch")
    block = VELS // (blocks * pairs)
    slot = jnp.arange(VELS, dtype=jnp.int32)
    to_member = (member + slot // (blocks * block)) % pairs
    to_group = (group + slot // block % blocks) % blocks
    order = (to_group * pairs + to_member) * block + slot % block
    first = (member * epochs).astype(jnp.int32)[None]
    rows_out = -(-(tile + 2 * REACH) // 16) * 16
    smem = pl.BlockSpec(memory_space=pltpu.SMEM)
    vmem = pl.BlockSpec(memory_space=pltpu.VMEM)
    partial = pl.pallas_call(
        functools.partial(stack_kernel, tile),
        out_shape=jax.ShapeDtypeStruct((VELS, 2, tile, tile), jnp.bfloat16),
        in_specs=[smem, smem, smem, smem, vmem, vmem],
        out_specs=vmem,
        scratch_shapes=[
            pltpu.VMEM((2 * epochs, rows_out, LANES), jnp.float32),
            pltpu.VMEM((2 * epochs, rows_out, LANES), jnp.float32),
        ],
        compiler_params=pltpu.CompilerParams(vmem_limit_bytes=48 * 2**20),
    )(offsets, psf_sigma, order.astype(jnp.int32), first, own, halo)
    half = blocks * block
    sums = partial[:half].astype(jnp.float32)
    for away in range(1, pairs):
        came = shifted(partial[away * half : (away + 1) * half], "vel", away)
        sums = sums + came.astype(jnp.float32)
    total = sums[:block]
    for away in range(1, blocks):
        sent = sums[away * block : (away + 1) * block].astype(jnp.bfloat16)
        total = total + shifted(sent, "epoch", away).astype(jnp.float32)
    psi_sum = total[:, 0]
    phi_sum = jnp.maximum(total[:, 1], phi_floor)
    likelihood = psi_sum / jnp.sqrt(phi_sum)
    flux = psi_sum / phi_sum
    return (likelihood[:, None], flux[:, None])


def solution(mesh):
    placed = (
        P(("epoch", "vel"), ("field", "sky"), None, None),
        P(("epoch", "vel"), ("field", "sky"), None, None),
        P(("epoch", "vel"), ("field", "sky")),
        P(("field", "epoch", "vel")),
        P(None, None, "epoch"),
    )
    return jax.shard_map(
        on_device,
        mesh=mesh,
        in_specs=placed,
        out_specs=(
            P(("epoch", "vel"), ("field", "sky"), None, None),
            P(("epoch", "vel"), ("field", "sky"), None, None),
        ),
        check_vma=False,
    )
```

time: 642 us -> 46.7 us (0.07)
  local copies, waits for them, and re-layouts: 522 us -> 2.1 us
  waiting for transfers between devices: 42.8 us -> 14.9 us
  matrix products: 20.2 us -> 0 us
  other arithmetic: 23.9 us -> 4.43 us
  Pallas kernels: 0 us -> 17.5 us
  between operations: 14.2 us -> 0.74 us
  loops' own time: 7.93 us -> 0 us
    gather x768 -> x0, local copies, waits for them, and re-layouts: 478 us -> none
    squeeze x32 -> x0, local copies, waits for them, and re-layouts: 31.8 us -> none  [accumulate(): epoch_map = lax.dynamic_index_in_dim(corrected, epoch_id, 0, keepdims=False)]
    reduce_scatter x1 -> x0, waiting for transfers between devices: 21.7 us -> none  [on_device(): lax.psum_scatter(stack_block(shared, offsets, chosen), 'epoch', scatter_d...]
    all_gather x1 -> x0, waiting for transfers between devices: 21 us -> none  [on_device(): shared = lax.all_gather(corrected, 'vel', axis=0, tiled=True)]
    dot_general x1 -> x0, matrix products: 20.2 us -> none  [on_device(): jnp.einsum('emox,emxp->emop', rows_done, banded, preferred_element_type=j...]
    pallas_call x0 -> x1, Pallas kernels: none -> 17.5 us  [on_device(): pl.pallas_call(functools.partial(stack_kernel, tile), out_shape=jax.Shape...]
    ppermute x4, waiting for transfers between devices: 0.01 us -> 14.9 us  [shifted(): return lax.ppermute(block, axis, route)]
    add x33 -> x3, other arithmetic: 11.1 us -> 0.2 us  [the longest x1 0.13 us: on_device(): sums = sums + came.astype(jnp.float32)]
  transfers between devices with their start and end apart: 6 -> 4, of which waited for: 2 -> 4; matrix products, arithmetic and copies ran while one was open for 3% -> 2% of each run, Pallas kernels for 0% -> 0%
where the time goes in v1:
time: 46.7 us; the launch traced here: 46.5 us
  Pallas kernels  17.5 us (37%)
  waiting for transfers between devices  14.9 us (32%)
  starting transfers between devices  6.81 us (15%)
  other arithmetic  4.43 us (9%)
  local copies, waits for them, and re-layouts  2.1 us (4%)
  between operations  0.74 us (2%)
    pallas_call x1, Pallas kernels, on_device(): pl.pallas_call(functools.partial(stack_kernel, tile), out_shape=jax.Shape...  17.5 us
    ppermute x4, waiting for transfers between devices, shifted(): return lax.ppermute(block, axis, route)  14.9 us
    ppermute x4, starting transfers between devices, shifted(): return lax.ppermute(block, axis, route)  6.81 us
    convert_element_type x1, other arithmetic, on_device(): scaled.astype(jnp.bfloat16)  1.57 us
    another operation x2, other arithmetic, on_device(): jnp.stack([scaled.astype(jnp.bfloat16), inverse.astype(jnp.bfloat16)], ax...  1.11 us
  transfers between devices with their start and end apart: 4, of which 4 were waited for; matrix products, arithmetic and copies ran while one was open for 2% of the time, Pallas kernels for 0%

profile of v1, /device:TPU:0, one launch (start us, length us, event | category | flops | bytes accessed | tf_op | source)
XLA Modules:
  0.0 46.5 jit_solution(16554850730647277062)
XLA Ops:
  0.6 0.7 %convert_bitcast_fusion = f32[16]{0:T(128)S(1)} fusion(s32[16,1]{0,1:T(1,128)} %param.7), kind=kLoop, calls=%fused_computation.47 | loop fusion | flops 16 | bytes 128 | tf_op jit(solution)/shard_map/convert_element_type | solution.py:108
  1.3 1.6 %fusion.1 = (bf16[16,1,128,128]{3,2,1,0:T(8,128)(2,1)S(1)}, bf16[16,1,128,128]{3,2,1,0:T(8,128)(2,1)S(1)}) fusion(bf16[16,1,128,128]{3,2,1,0:T(8,128)(2,1)} %param.6, bf16[16,1,128,128]{3,2,1,0:T(8,128)(2,1)} %param.5, f32[16]{0:T(128)S(1)} %convert_bitcast_fusion), kind=kLoop, calls=%fused_computation.8 | loop fusion | flops 1835008 | bytes 2097216 | tf_op jit(solution)/shard_map/convert_element_type | solution.py:111
  2.9 0.4 fusion.3
  3.3 0.4 copy.15
  3.7 3.1 %collective-permute-start = (bf16[16,2,128,19]{2,0,3,1:T(8,128)(2,1)S(1)}, bf16[16,2,128,19]{2,0,3,1:T(8,128)(2,1)S(1)}, u32[]{:S(2)}, u32[]{:S(2)}) collective-permute-start(bf16[16,2,128,19]{2,0,3,1:T(8,128)(2,1)S(1)} %copy.15), channel_id=1, source_target_pairs={{12,0},{0,4},{4,8},{8,12},{13,1},{1,5},{5,9},{9,13},{14,2},{2,6},{... | collective-permute-start | bytes 466952 | tf_op jit(solution)/shard_map/ppermute | solution.py:23
  6.8 0.4 copy.16
  7.2 2.1 %collective-permute-start.1 = (bf16[16,2,128,19]{2,0,3,1:T(8,128)(2,1)S(1)}, bf16[16,2,128,19]{2,0,3,1:T(8,128)(2,1)S(1)}, u32[]{:S(2)}, u32[]{:S(2)}) collective-permute-start(bf16[16,2,128,19]{2,0,3,1:T(8,128)(2,1)S(1)} %copy.16), channel_id=1, source_target_pairs={{4,0},{8,4},{12,8},{0,12},{5,1},{9,5},{13,9},{1,13},{6,2},{10,6},{... | collective-permute-start | bytes 466952 | tf_op jit(solution)/shard_map/ppermute | solution.py:23
  9.3 0.1 pad.2.clone
  9.4 4.3 %collective-permute-done = bf16[16,2,128,19]{2,0,3,1:T(8,128)(2,1)S(1)} collective-permute-done((bf16[16,2,128,19]{2,0,3,1:T(8,128)(2,1)S(1)}, bf16[16,2,128,19]{2,0,3,1:T(8,128)(2,1)S(1)}, u32[]{:S(2)}, u32[]{:S(2)}) %collective-permute-start) | collective-permute-done | bytes 155680 | tf_op jit(solution)/shard_map/ppermute | solution.py:23
  13.8 0.5 %copy.17 = bf16[16,2,128,19]{3,2,1,0:T(8,128)(2,1)S(1)} copy(bf16[16,2,128,19]{2,0,3,1:T(8,128)(2,1)S(1)} %broadcast_select_fusion.1) | data formatting | bytes 311296 | tf_op jit(solution)/shard_map/jit(_where)/select_n | solution.py:117
  14.3 1.8 %collective-permute-done.1 = bf16[16,2,128,19]{2,0,3,1:T(8,128)(2,1)S(1)} collective-permute-done((bf16[16,2,128,19]{2,0,3,1:T(8,128)(2,1)S(1)}, bf16[16,2,128,19]{2,0,3,1:T(8,128)(2,1)S(1)}, u32[]{:S(2)}, u32[]{:S(2)}) %collective-permute-start.1) | collective-permute-done | bytes 155680 | tf_op jit(solution)/shard_map/ppermute | solution.py:23
  16.1 0.5 %copy.18 = bf16[16,2,128,19]{3,2,1,0:T(8,128)(2,1)S(1)} copy(bf16[16,2,128,19]{2,0,3,1:T(8,128)(2,1)S(1)} %broadcast_select_fusion) | data formatting | bytes 311296 | tf_op jit(solution)/shard_map/jit(_where)/select_n | solution.py:118
  16.6 0.0 copy-start
  16.7 0.0 copy-start.1
  16.7 0.7 %pad_maximum_fusion = (bf16[16,2,128,128]{3,2,1,0:T(8,128)(2,1)S(1)}, bf16[16,2,128,128]{3,2,1,0:T(8,128)(2,1)S(1)}) fusion(bf16[16,1,128,128]{3,2,1,0:T(8,128)(2,1)S(1)} %get-tuple-element.5, bf16[16,1,128,128]{3,2,1,0:T(8,128)(2,1)S(1)} %get-tuple-element.4, bf16[128]{0:T(256)(128)(2,1)S(1)} %pad.2.clone, bf16[16,2,128,19]{3,2,1,0:T(8,128)(2,1)S(1)} %copy.18, ...), kind=kLoop, calls=%fused_computation.2 | loop fusion | flops 5242880 | bytes 3457280 | tf_op jit(solution)/shard_map/stack | solution.py:111
  17.4 0.0 copy-done
  17.4 0.0 copy-done.1
  17.4 17.5 %shard_map.68 = bf16[16,2,128,128]{3,2,1,0:T(8,128)(2,1)S(1)} custom-call(s32[2,16,32]{2,1,0:T(8,128)S(1)} %copy-done, f32[16]{0:T(128)S(1)} %copy-done.1, s32[16]{0:T(128)S(1)} %fusion.5.order, s32[1]{0:T(128)} %bitcast.first, bf16[16,2,128,128]{3,2,1,0:T(8,128)(2,1)S(1)} %get-tuple-element.8.own, bf16[16,2,128,128]{3,2,1,0:T(8,128)(2,1)S(1)} %get-tuple-element.9.halo), custom_call_target="tpu_custom_call" | custom-call | tf_op jit(solution)/shard_map/pallas_call | solution.py:143
  35.0 0.1 collective-permute-start.2
  35.1 1.9 %collective-permute-done.2 = bf16[8,2,128,128]{3,2,1,0:T(8,128)(2,1)S(1)} collective-permute-done((bf16[8,2,128,128]{3,2,1,0:T(8,128)(2,1)S(1)}, bf16[8,2,128,128]{3,2,1,0:T(8,128)(2,1)S(1)}, u32[]{:S(2)}, u32[]{:S(2)}) %collective-permute-start.2) | collective-permute-done | bytes 524320 | tf_op jit(solution)/shard_map/ppermute | solution.py:23
  37.0 0.1 convert_add_fusion
  37.2 1.6 %collective-permute-start.3 = (bf16[4,2,128,128]{3,2,1,0:T(8,128)(2,1)S(1)}, bf16[4,2,128,128]{3,2,1,0:T(8,128)(2,1)S(1)}, u32[]{:S(2)}, u32[]{:S(2)}) collective-permute-start(bf16[4,2,128,128]{3,2,1,0:T(8,128)(2,1)S(1)} %slice.65), channel_id=1, source_target_pairs={{2,0},{0,2},{3,1},{1,3},{6,4},{4,6},{7,5},{5,7},{10,8},{8,10},{11,... | collective-permute-start | bytes 786440 | tf_op jit(solution)/shard_map/ppermute | solution.py:23
  38.7 6.9 %collective-permute-done.3 = bf16[4,2,128,128]{3,2,1,0:T(8,128)(2,1)S(1)} collective-permute-done((bf16[4,2,128,128]{3,2,1,0:T(8,128)(2,1)S(1)}, bf16[4,2,128,128]{3,2,1,0:T(8,128)(2,1)S(1)}, u32[]{:S(2)}, u32[]{:S(2)}) %collective-permute-start.3) | collective-permute-done | bytes 262176 | tf_op jit(solution)/shard_map/ppermute | solution.py:23
  45.6 0.1 slice_add_fusion
  45.6 0.9 %slice_divide_fusion = (f32[4,1,128,128]{3,2,1,0:T(8,128)}, f32[4,1,128,128]{3,2,1,0:T(8,128)}) fusion(f32[4,2,128,128]{3,2,1,0:T(8,128)S(1)} %slice_add_fusion), kind=kLoop, calls=%fused_computation.18 | loop fusion | flops 196608 | bytes 1048576 | tf_op jit(solution)/shard_map/div | solution.py:166
  (6 shorter events, 0.1 us)
Async XLA Ops:
  3.7 10.0 %collective-permute-start = (bf16[16,2,128,19]{2,0,3,1:T(8,128)(2,1)S(1)}, bf16[16,2,128,19]{2,0,3,1:T(8,128)(2,1)S(1)}, u32[]{:S(2)}, u32[]{:S(2)}) collective-permute-start(bf16[16,2,128,19]{2,0,3,1:T(8,128)(2,1)S(1)} %copy.15), channel_id=1, source_target_pairs={{12,0},{0,4},{4,8},{8,12},{13,1},{1,5},{5,9},{9,13},{14,2},{2,6},{... | collective-permute-start | bytes 466952 | tf_op jit(solution)/shard_map/ppermute | solution.py:23
  7.2 8.9 %collective-permute-start.1 = (bf16[16,2,128,19]{2,0,3,1:T(8,128)(2,1)S(1)}, bf16[16,2,128,19]{2,0,3,1:T(8,128)(2,1)S(1)}, u32[]{:S(2)}, u32[]{:S(2)}) collective-permute-start(bf16[16,2,128,19]{2,0,3,1:T(8,128)(2,1)S(1)} %copy.16), channel_id=1, source_target_pairs={{4,0},{8,4},{12,8},{0,12},{5,1},{9,5},{13,9},{1,13},{6,2},{10,6},{... | collective-permute-start | bytes 466952 | tf_op jit(solution)/shard_map/ppermute | solution.py:23
  16.6 0.7 %copy-start = (s32[2,16,32]{2,1,0:T(8,128)S(1)}, s32[2,16,32]{2,1,0:T(8,128)}, u32[]{:S(2)}) copy-start(s32[2,16,32]{2,1,0:T(8,128)} %offsets.1) | copy-start | bytes 12292
  16.7 0.7 %copy-start.1 = (f32[16]{0:T(128)S(1)}, f32[16]{0:T(128)}, u32[]{:S(2)}) copy-start(f32[16]{0:T(128)} %sigmas.1) | copy-start | bytes 196
  35.0 2.0 %collective-permute-start.2 = (bf16[8,2,128,128]{3,2,1,0:T(8,128)(2,1)S(1)}, bf16[8,2,128,128]{3,2,1,0:T(8,128)(2,1)S(1)}, u32[]{:S(2)}, u32[]{:S(2)}) collective-permute-start(bf16[8,2,128,128]{3,2,1,0:T(8,128)(2,1)S(1)} %slice.38), channel_id=1, source_target_pairs={{1,0},{0,1},{3,2},{2,3},{5,4},{4,5},{7,6},{6,7},{9,8},{8,9},{11,10... | collective-permute-start | bytes 1572872 | tf_op jit(solution)/shard_map/ppermute | solution.py:23
  37.2 8.4 %collective-permute-start.3 = (bf16[4,2,128,128]{3,2,1,0:T(8,128)(2,1)S(1)}, bf16[4,2,128,128]{3,2,1,0:T(8,128)(2,1)S(1)}, u32[]{:S(2)}, u32[]{:S(2)}) collective-permute-start(bf16[4,2,128,128]{3,2,1,0:T(8,128)(2,1)S(1)} %slice.65), channel_id=1, source_target_pairs={{2,0},{0,2},{3,1},{1,3},{6,4},{4,6},{7,5},{5,7},{10,8},{8,10},{11,... | collective-permute-start | bytes 786440 | tf_op jit(solution)/shard_map/ppermute | solution.py:23

commit v2 on v1

v2 whole, which is shorter than its diff:
```python
import functools

import jax
import jax.numpy as jnp
from jax import lax
from jax.experimental import pallas as pl
from jax.experimental.pallas import tpu as pltpu
from jax.sharding import PartitionSpec as P

VELS = 16
REACH = 12
PSFR = 7
GRID_X = 4
MARGIN = REACH + PSFR
LANES = 128

phi_floor = 0.25


def shifted(block, axis, distance):
    devices = range(lax.axis_size(axis))
    route = [((i - distance) % len(devices), i) for i in devices]
    return lax.ppermute(block, axis, route)


def positions(index, tile):
    return jnp.where(
        index < tile,
        index,
        jnp.where(
            index < tile + MARGIN,
            index - tile - MARGIN,
            jnp.where(index < tile + 2 * MARGIN, index - MARGIN, 4 * tile),
        ),
    )


FAR = -1.0e9


def exponents(distance):
    away = distance.astype(jnp.float32)
    return jnp.where(jnp.abs(distance) <= PSFR, -0.5 * away * away, FAR)


def fused_kernel(plan, *refs):
    tile, sky, blocks, block, epochs, exchange = plan
    if exchange:
        (offsets, sigmas, valid, images, variances, likelihood, flux, plane_a, plane_b, row_q,
         own_q, side_q, bands, send_v, recv_v, send_x, recv_x, keep, sv, rv, sx, rx,
         own, building, sent_sides, came_sides, sz, rz) = refs
    else:
        (offsets, sigmas, own, halo, likelihood, flux, plane_a, plane_b, row_q,
         own_q, side_q, bands, send_v, recv_v, send_x, recv_x, keep, sv, rv, sx, rx) = refs
    maps = 2
    slots = LANES // MARGIN
    rows_in = row_q.shape[1]
    rows_out = plane_a.shape[1]
    width = 2 * LANES
    mesh_id = pl.DeviceIdType.MESH
    me = lax.axis_index("sky")
    group = lax.axis_index("epoch")
    member = lax.axis_index("vel")
    column = lax.rem(lax.rem(me + GRID_X // 2, sky), GRID_X)
    before = lax.rem(me + sky - 1, sky)
    after = lax.rem(me + 1, sky)
    partner = 1 - member

    barrier = pltpu.get_barrier_semaphore()
    greeted = 1
    pl.semaphore_signal(barrier, inc=1, device_id={"vel": partner}, device_id_type=mesh_id)
    for a in range(1, blocks):
        peer = lax.rem(group + a, blocks)
        pl.semaphore_signal(barrier, inc=1, device_id={"epoch": peer}, device_id_type=mesh_id)
        greeted += 1
    if exchange:
        for other in (before, after):
            pl.semaphore_signal(barrier, inc=1, device_id={"sky": other}, device_id_type=mesh_id)
            greeted += 1

    if exchange:
        groups = sent_sides.shape[1]
        lane = lax.broadcasted_iota(jnp.int32, (tile, LANES), 1)

        def side_copy(to_after, g):
            return pltpu.make_async_remote_copy(
                src_ref=sent_sides.at[to_after, g],
                dst_ref=came_sides.at[to_after, g],
                send_sem=sz.at[to_after, g],
                recv_sem=rz.at[to_after, g],
                device_id={"sky": after if to_after else before},
                device_id_type=mesh_id,
            )

        building[...] = jnp.zeros_like(building)

        @pl.when(column == 0)
        def _():
            came_sides[1] = jnp.zeros_like(came_sides[1])

        @pl.when(column == GRID_X - 1)
        def _():
            came_sides[0] = jnp.zeros_like(came_sides[0])

        pl.semaphore_wait(barrier, greeted)

        def weigh(e, carry):
            s = lax.rem(e, slots)
            g = e // slots
            usable = valid[e, 0].astype(jnp.float32)
            inverse = usable / variances[e, 0].astype(jnp.float32)
            scaled = images[e, 0].astype(jnp.float32) * inverse
            to_slot = MARGIN * s
            to_mirror = MARGIN * (slots - 1 - s)
            for m, field in enumerate((scaled, inverse)):
                own[e, m] = field.astype(jnp.bfloat16)
                low = pltpu.roll(field, to_mirror, axis=1)
                high = pltpu.roll(field, to_slot + MARGIN, axis=1)
                at_low = (lane >= to_mirror) & (lane < to_mirror + MARGIN)
                at_high = (lane >= to_slot) & (lane < to_slot + MARGIN)
                building[0, m] = jnp.where(at_low, low, building[0, m])
                building[1, m] = jnp.where(at_high, high, building[1, m])

            @pl.when((s == slots - 1) | (e == epochs - 1))
            def _():
                sent_sides[0, g] = building[0].astype(jnp.bfloat16)
                sent_sides[1, g] = building[1].astype(jnp.bfloat16)

                @pl.when(column > 0)
                def _():
                    side_copy(0, g).start()

                @pl.when(column < GRID_X - 1)
                def _():
                    side_copy(1, g).start()

            return carry

        lax.fori_loop(0, epochs, weigh, 0)
    else:
        pl.semaphore_wait(barrier, greeted)

    shape = (rows_out, rows_in)
    row_q[...] = exponents(
        positions(lax.broadcasted_iota(jnp.int32, shape, 1), tile)
        - lax.broadcasted_iota(jnp.int32, shape, 0) + REACH
    )
    shape = (LANES, width)
    held = lax.broadcasted_iota(jnp.int32, shape, 0)
    shifted_out = lax.broadcasted_iota(jnp.int32, shape, 1) - REACH
    own_q[...] = exponents(held - shifted_out)
    if exchange:
        for s in range(slots):
            low, high = MARGIN * s, MARGIN * (slots - 1 - s)
            pixel = jnp.where(
                (held >= low) & (held < low + MARGIN),
                held - low - MARGIN,
                jnp.where((held >= high) & (held < high + MARGIN), held - high + tile, 4 * tile),
            )
            side_q[s] = exponents(pixel - shifted_out)
    else:
        side_q[0] = exponents(positions(held + tile, tile) - shifted_out)

    def correlate(e, carry):
        sigma = jnp.full((8, LANES), sigmas[e], jnp.float32)
        power = 1.0 / (sigma * sigma)
        tap = lax.broadcasted_iota(jnp.int32, (8, LANES), 1) - PSFR
        norm = jnp.sum(jnp.exp(exponents(tap) * power), axis=1, keepdims=True)
        scale = (1.0 / norm)[:1]
        power = power[:1, :1]

        def both(q):
            profile = jnp.exp(q * power) * scale
            return profile.astype(jnp.bfloat16), (profile * profile).astype(jnp.bfloat16)

        row_bands = both(row_q[...])
        s = lax.rem(e, slots) if exchange else 0
        for part, q in enumerate((own_q[...], side_q[s])):
            for m, made in enumerate(both(q)):
                bands[m, part * LANES : (part + 1) * LANES] = made
        if exchange:
            g = e // slots

            @pl.when(s == 0)
            def _():
                @pl.when(column < GRID_X - 1)
                def _():
                    side_copy(0, g).wait_recv()

                @pl.when(column > 0)
                def _():
                    side_copy(1, g).wait_recv()

            lane = lax.broadcasted_iota(jnp.int32, (tile, LANES), 1)
            in_slot = (lane >= MARGIN * s) & (lane < MARGIN * s + MARGIN)
        for m in range(maps):
            if exchange:
                side = jnp.where(
                    in_slot,
                    came_sides[1, g, m].astype(jnp.float32),
                    came_sides[0, g, m].astype(jnp.float32),
                ).astype(jnp.bfloat16)
            else:
                side = halo[e, m]
            held = jnp.concatenate([own[e, m], side], axis=1)
            rows = jnp.dot(row_bands[m], held, preferred_element_type=jnp.float32)
            done = jnp.dot(
                rows.astype(jnp.bfloat16), bands[m], preferred_element_type=jnp.float32
            )
            plane_a[maps * e + m] = done[:, :LANES]
            plane_b[maps * e + m] = done[:, LANES:]
        return carry

    lax.fori_loop(0, epochs, correlate, 0)

    def vel_copy(at):
        return pltpu.make_async_remote_copy(
            src_ref=send_v.at[at], dst_ref=recv_v.at[at], send_sem=sv.at[at], recv_sem=rv.at[at],
            device_id={"vel": partner}, device_id_type=mesh_id,
        )

    def epoch_copy(at):
        peer = lax.rem(group + 1 + at // block, blocks)
        return pltpu.make_async_remote_copy(
            src_ref=send_x.at[at], dst_ref=recv_x.at[at], send_sem=sx.at[at], recv_sem=rx.at[at],
            device_id={"epoch": peer}, device_id_type=mesh_id,
        )

    first = member * epochs

    def stack(slot, carry):
        a = blocks - 1 - slot // (2 * block)
        b = 1 - lax.rem(slot // block, 2)
        j = lax.rem(slot, block)
        at = a * block + j
        k = (lax.rem(group + a, blocks) * 2 + lax.rem(member + b, 2)) * block + j
        lane = lax.broadcasted_iota(jnp.int32, (tile, LANES), 1)
        summed = [jnp.zeros((tile, LANES), jnp.float32) for _ in range(maps)]
        for e in range(epochs):
            down = offsets[0, k, first + e] + REACH
            right = offsets[1, k, first + e] + REACH
            for m in range(maps):
                left_part = plane_a[maps * e + m, pl.ds(down, tile), :]
                right_part = plane_b[maps * e + m, pl.ds(down, tile), :]
                merged = jnp.where(lane >= right, left_part, right_part)
                summed[m] += pltpu.roll(merged, LANES - right, axis=1)
        for m in range(maps):
            keep[j, m] = summed[m]

        @pl.when(b == 1)
        def _():
            send_v[at] = keep[j].astype(jnp.bfloat16)
            vel_copy(at).start()

        @pl.when(b == 0)
        def _():
            vel_copy(at).wait_recv()
            keep[j] = keep[j] + recv_v[at].astype(jnp.float32)

            @pl.when(a > 0)
            def _():
                send_x[at - block] = keep[j].astype(jnp.bfloat16)
                epoch_copy(at - block).start()

        return carry

    lax.fori_loop(0, 2 * blocks * block, stack, 0)

    def finish(j, carry):
        total = keep[j]
        for a in range(1, blocks):
            at = (a - 1) * block + j
            epoch_copy(at).wait_recv()
            total = total + recv_x[at].astype(jnp.float32)
        phi = jnp.maximum(total[1], phi_floor)
        likelihood[j, 0] = total[0] / jnp.sqrt(phi)
        flux[j, 0] = total[0] / phi
        return carry

    lax.fori_loop(0, block, finish, 0)

    def drain_v(at, carry):
        vel_copy(at).wait_send()
        return carry

    lax.fori_loop(0, blocks * block, drain_v, 0)

    def drain_x(at, carry):
        epoch_copy(at).wait_send()
        return carry

    lax.fori_loop(0, (blocks - 1) * block, drain_x, 0)
    if exchange:

        def drain_z(g, carry):
            @pl.when(column > 0)
            def _():
                side_copy(0, g).wait_send()

            @pl.when(column < GRID_X - 1)
            def _():
                side_copy(1, g).wait_send()

            return carry

        lax.fori_loop(0, groups, drain_z, 0)


def strips(own, tile_count, tile):
    position = (lax.axis_index("sky") + GRID_X // 2) % tile_count
    column = position % GRID_X
    left = shifted(own[..., tile - MARGIN :], "sky", 1)
    right = shifted(own[..., :MARGIN], "sky", -1)
    left = jnp.where(column > 0, left, jnp.zeros_like(left))
    right = jnp.where(column < GRID_X - 1, right, jnp.zeros_like(right))
    blank = jnp.zeros(own.shape[:3] + (LANES - 2 * MARGIN,), jnp.bfloat16)
    both = jnp.concatenate([own, left, right, blank], axis=3)
    upper = shifted(both[:, :, tile - MARGIN :], "sky", GRID_X)
    lower = shifted(both[:, :, :MARGIN], "sky", -GRID_X)
    upper = jnp.where(position >= GRID_X, upper, jnp.zeros_like(upper))
    lower = jnp.where(position < tile_count - GRID_X, lower, jnp.zeros_like(lower))
    blank = jnp.zeros(both.shape[:2] + (LANES - 2 * MARGIN, both.shape[3]), jnp.bfloat16)
    both = jnp.concatenate([both, upper, lower, blank], axis=2)
    return both[..., :tile], both[..., tile:]


def on_device(images, variances, valid, psf_sigma, offsets):
    epochs = images.shape[0]
    tile = images.shape[-1]
    sky = lax.axis_size("sky")
    blocks = lax.axis_size("epoch")
    block = VELS // (blocks * lax.axis_size("vel"))
    exchange = sky == GRID_X
    rows_out = -(-(tile + 2 * REACH) // 16) * 16
    slots = LANES // MARGIN
    smem = pl.BlockSpec(memory_space=pltpu.SMEM)
    vmem = pl.BlockSpec(memory_space=pltpu.VMEM)
    dma = pltpu.SemaphoreType.DMA
    half = blocks * block
    far = max(1, (blocks - 1) * block)
    scratch = [
        pltpu.VMEM((2 * epochs, rows_out, LANES), jnp.float32),
        pltpu.VMEM((2 * epochs, rows_out, LANES), jnp.float32),
        pltpu.VMEM((rows_out, tile if exchange else tile + LANES), jnp.float32),
        pltpu.VMEM((LANES, 2 * LANES), jnp.float32),
        pltpu.VMEM((slots if exchange else 1, LANES, 2 * LANES), jnp.float32),
        pltpu.VMEM((2, 2 * LANES, 2 * LANES), jnp.bfloat16),
        pltpu.VMEM((half, 2, tile, tile), jnp.bfloat16),
        pltpu.VMEM((half, 2, tile, tile), jnp.bfloat16),
        pltpu.VMEM((far, 2, tile, tile), jnp.bfloat16),
        pltpu.VMEM((far, 2, tile, tile), jnp.bfloat16),
        pltpu.VMEM((block, 2, tile, tile), jnp.float32),
        dma((half,)), dma((half,)), dma((far,)), dma((far,)),
    ]
    if exchange:
        groups = -(-epochs // slots)
        scratch += [
            pltpu.VMEM((epochs, 2, tile, tile), jnp.bfloat16),
            pltpu.VMEM((2, 2, tile, LANES), jnp.float32),
            pltpu.VMEM((2, groups, 2, tile, LANES), jnp.bfloat16),
            pltpu.VMEM((2, groups, 2, tile, LANES), jnp.bfloat16),
            dma((2, groups)), dma((2, groups)),
        ]
        operands = (offsets, psf_sigma, valid, images, variances)
        in_specs = [smem, smem, smem, vmem, vmem]
    else:
        usable = valid[:, 0].astype(jnp.float32)[:, None, None]
        inverse = usable / variances[:, 0].astype(jnp.float32)
        scaled = images[:, 0].astype(jnp.float32) * inverse
        own = jnp.stack([scaled.astype(jnp.bfloat16), inverse.astype(jnp.bfloat16)], axis=1)
        operands = (offsets, psf_sigma) + strips(own, sky, tile)
        in_specs = [smem, smem, vmem, vmem]
    out = jax.ShapeDtypeStruct((block, 1, tile, tile), jnp.float32)
    return pl.pallas_call(
        functools.partial(fused_kernel, (tile, sky, blocks, block, epochs, exchange)),
        out_shape=(out, out),
        in_specs=in_specs,
        out_specs=(vmem, vmem),
        scratch_shapes=scratch,
        compiler_params=pltpu.CompilerParams(
            collective_id=0, has_side_effects=True, vmem_limit_bytes=56 * 2**20
        ),
    )(*operands)


def solution(mesh):
    placed = (
        P(("epoch", "vel"), ("field", "sky"), None, None),
        P(("epoch", "vel"), ("field", "sky"), None, None),
        P(("epoch", "vel"), ("field", "sky")),
        P(("field", "epoch", "vel")),
        P(None, None, "epoch"),
    )
    return jax.shard_map(
        on_device,
        mesh=mesh,
        in_specs=placed,
        out_specs=(
            P(("epoch", "vel"), ("field", "sky"), None, None),
            P(("epoch", "vel"), ("field", "sky"), None, None),
        ),
        check_vma=False,
    )
```

time: 46.7 us -> 37.2 us (0.80)
  Pallas kernels: 17.5 us -> 32.6 us
  waiting for transfers between devices: 14.9 us -> 0 us
  starting transfers between devices: 6.81 us -> 0 us
  other arithmetic: 4.43 us -> 0 us
  local copies, waits for them, and re-layouts: 2.1 us -> 3.75 us
    pallas_call x1, Pallas kernels: 17.5 us -> 32.6 us  [on_device(): pl.pallas_call(functools.partial(fused_kernel, (tile, sky, blocks, block,...]
    ppermute x4 -> x0, waiting for transfers between devices: 14.9 us -> none  [shifted(): return lax.ppermute(block, axis, route)]
    ppermute x4 -> x0, starting transfers between devices: 6.81 us -> none  [shifted(): return lax.ppermute(block, axis, route)]
    unnamed x4 -> x5, local copies, waits for them, and re-layouts: 0.01 us -> 3.75 us
    convert_element_type x2 -> x0, other arithmetic: 2.23 us -> none  [the longest x1 1.57 us: on_device(): scaled.astype(jnp.bfloat16)]
    another operation x2 -> x0, other arithmetic: 1.11 us -> none  [on_device(): jnp.stack([scaled.astype(jnp.bfloat16), inverse.astype(jnp.bfloat16)], ax...]
    select_n x2 -> x0, local copies, waits for them, and re-layouts: 1.07 us -> none  [the longest x1 0.53 us: on_device(): left = jnp.where(column > 0, left, jnp.zeros_like(left))]
    slice x4 -> x0, local copies, waits for them, and re-layouts: 0.94 us -> none  [the longest x1 0.44 us: on_device(): left = shifted(own[..., tile - MARGIN:], 'sky', 1)]
  transfers between devices with their start and end apart: 4 -> 0, of which waited for: 4 -> 0; matrix products, arithmetic and copies ran while one was open for 2% -> 0% of each run, Pallas kernels for 0% -> 0%
where the time goes in v2:
time: 37.2 us; the launch traced here: 37 us
  Pallas kernels  32.6 us (88%)
  local copies, waits for them, and re-layouts  3.75 us (10%)
  between operations  0.65 us (2%)
    pallas_call x1, Pallas kernels, on_device(): pl.pallas_call(functools.partial(fused_kernel, (tile, sky, blocks, block,...  32.6 us
    unnamed x5, local copies, waits for them, and re-layouts  3.75 us

profile of v2, /device:TPU:0, one launch (start us, length us, event | category | flops | bytes accessed | tf_op | source)
XLA Modules:
  0.0 37.0 jit_solution(514095975534040851)
XLA Ops:
  0.6 1.3 %copy.7.refs_2_ = s32[16,1]{1,0:T(8,128)} copy(s32[16,1]{0,1:T(1,128)} %param.7) | data formatting | bytes 128 | tf_op args[2]
  2.0 32.6 %shard_map.68 = (f32[4,1,128,128]{3,2,1,0:T(8,128)}, f32[4,1,128,128]{3,2,1,0:T(8,128)}) custom-call(s32[2,16,32]{2,1,0:T(8,128)} %refs_0_.1, f32[16]{0:T(128)} %refs_1_.1, s32[16,1]{1,0:T(8,128)} %copy.7.refs_2_, bf16[16,1,128,128]{3,2,1,0:T(8,128)(2,1)} %refs_3_.1, bf16[16,1,128,128]{3,2,1,0:T(8,128)(2,1)} %refs_4_.1), custom_call_target="tpu_custom_call" | custom-call | tf_op jit(solution)/shard_map/pallas_call | solution.py:374
  34.6 0.0 copy-start
  34.6 1.7 %copy.10 = f32[4,1,128,128]{3,2,1,0:T(8,128)} copy(f32[4,1,128,128]{3,2,1,0:T(8,128)} %get-tuple-element.4) | data formatting | bytes 524288
  36.3 0.0 copy-done
  36.3 0.7 %copy.11 = f32[4,1,128,128]{3,2,1,0:T(8,128)} copy(f32[4,1,128,128]{3,2,1,0:T(8,128)S(1)} %copy-done) | data formatting | bytes 524288
Async XLA Ops:
  34.6 1.7 %copy-start = (f32[4,1,128,128]{3,2,1,0:T(8,128)S(1)}, f32[4,1,128,128]{3,2,1,0:T(8,128)}, u32[]{:S(2)}) copy-start(f32[4,1,128,128]{3,2,1,0:T(8,128)} %get-tuple-element.5) | copy-start | bytes 786436

commit v3 on v2

--- a/solution.py
+++ b/solution.py
@@ -44,13 +44,13 @@
 
 
 def fused_kernel(plan, *refs):
-    tile, sky, blocks, block, epochs, exchange = plan
-    if exchange:
-        (offsets, sigmas, valid, images, variances, likelihood, flux, plane_a, plane_b, row_q,
+    tile, sky, blocks, block, epochs, runs, exchange = plan
+    if exchange:
+        (offsets, sigmas, valid, images, variances, out, plane_a, plane_b, ends, row_q,
          own_q, side_q, bands, send_v, recv_v, send_x, recv_x, keep, sv, rv, sx, rx,
          own, building, sent_sides, came_sides, sz, rz) = refs
     else:
-        (offsets, sigmas, own, halo, likelihood, flux, plane_a, plane_b, row_q,
+        (offsets, sigmas, own, halo, out, plane_a, plane_b, ends, row_q,
          own_q, side_q, bands, send_v, recv_v, send_x, recv_x, keep, sv, rv, sx, rx) = refs
     maps = 2
     slots = LANES // MARGIN
@@ -107,7 +107,7 @@
         def weigh(e, carry):
             s = lax.rem(e, slots)
             g = e // slots
-            usable = valid[e, 0].astype(jnp.float32)
+            usable = valid[pl.ds(e, 1), :].astype(jnp.float32)
             inverse = usable / variances[e, 0].astype(jnp.float32)
             scaled = images[e, 0].astype(jnp.float32) * inverse
             to_slot = MARGIN * s
@@ -161,7 +161,22 @@
     else:
         side_q[0] = exponents(positions(held + tile, tile) - shifted_out)
 
-    def correlate(e, carry):
+    first = member * epochs
+
+    def count_runs(k, carry):
+        moved = []
+        for e in range(epochs):
+            down = jnp.abs(offsets[0, k, first + e] - offsets[0, k, first])
+            moved.append(down + jnp.abs(offsets[1, k, first + e] - offsets[1, k, first]))
+        for run in range(runs - 1):
+            ends[k, run] = sum((at <= run).astype(jnp.int32) for at in moved)
+        return carry
+
+    lax.fori_loop(0, VELS, count_runs, 0)
+    plane_a[:maps] = jnp.zeros_like(plane_a[:maps])
+    plane_b[:maps] = jnp.zeros_like(plane_b[:maps])
+
+    def correlate(e, turn):
         sigma = jnp.full((8, LANES), sigmas[e], jnp.float32)
         power = 1.0 / (sigma * sigma)
         tap = lax.broadcasted_iota(jnp.int32, (8, LANES), 1) - PSFR
@@ -177,20 +192,9 @@
         s = lax.rem(e, slots) if exchange else 0
         for part, q in enumerate((own_q[...], side_q[s])):
             for m, made in enumerate(both(q)):
-                bands[m, part * LANES : (part + 1) * LANES] = made
+                bands[turn, m, part * LANES : (part + 1) * LANES] = made
         if exchange:
             g = e // slots
-
-            @pl.when(s == 0)
-            def _():
-                @pl.when(column < GRID_X - 1)
-                def _():
-                    side_copy(0, g).wait_recv()
-
-                @pl.when(column > 0)
-                def _():
-                    side_copy(1, g).wait_recv()
-
             lane = lax.broadcasted_iota(jnp.int32, (tile, LANES), 1)
             in_slot = (lane >= MARGIN * s) & (lane < MARGIN * s + MARGIN)
         for m in range(maps):
@@ -205,13 +209,33 @@
             held = jnp.concatenate([own[e, m], side], axis=1)
             rows = jnp.dot(row_bands[m], held, preferred_element_type=jnp.float32)
             done = jnp.dot(
-                rows.astype(jnp.bfloat16), bands[m], preferred_element_type=jnp.float32
+                rows.astype(jnp.bfloat16), bands[turn, m], preferred_element_type=jnp.float32
             )
-            plane_a[maps * e + m] = done[:, :LANES]
-            plane_b[maps * e + m] = done[:, LANES:]
-        return carry
-
-    lax.fori_loop(0, epochs, correlate, 0)
+            at = maps * e + m
+            plane_a[at + maps] = plane_a[at] + done[:, :LANES]
+            plane_b[at + maps] = plane_b[at] + done[:, LANES:]
+
+    step = 2 if epochs % 2 == 0 and slots % 2 == 0 else 1
+
+    def several(i, carry):
+        for turn in range(step):
+            correlate(step * i + turn, turn)
+        return carry
+
+    if exchange:
+        for g in range(groups):
+
+            @pl.when(column < GRID_X - 1)
+            def _():
+                side_copy(0, g).wait_recv()
+
+            @pl.when(column > 0)
+            def _():
+                side_copy(1, g).wait_recv()
+
+            lax.fori_loop(g * slots // step, min((g + 1) * slots, epochs) // step, several, 0)
+    else:
+        lax.fori_loop(0, epochs // step, several, 0)
 
     def vel_copy(at):
         return pltpu.make_async_remote_copy(
@@ -226,41 +250,44 @@
             device_id={"epoch": peer}, device_id_type=mesh_id,
         )
 
-    first = member * epochs
-
     def stack(slot, carry):
         a = blocks - 1 - slot // (2 * block)
         b = 1 - lax.rem(slot // block, 2)
         j = lax.rem(slot, block)
-        at = a * block + j
+        place = a * block + j
         k = (lax.rem(group + a, blocks) * 2 + lax.rem(member + b, 2)) * block + j
         lane = lax.broadcasted_iota(jnp.int32, (tile, LANES), 1)
         summed = [jnp.zeros((tile, LANES), jnp.float32) for _ in range(maps)]
-        for e in range(epochs):
-            down = offsets[0, k, first + e] + REACH
-            right = offsets[1, k, first + e] + REACH
+        low = jnp.zeros((), jnp.int32)
+        for run in range(runs):
+            high = ends[k, run] if run < runs - 1 else epochs
+            at = first + jnp.minimum(low, epochs - 1)
+            down = offsets[0, k, at] + REACH
+            right = offsets[1, k, at] + REACH
+            rows = pl.ds(down, tile)
             for m in range(maps):
-                left_part = plane_a[maps * e + m, pl.ds(down, tile), :]
-                right_part = plane_b[maps * e + m, pl.ds(down, tile), :]
+                left_part = plane_a[maps * high + m, rows, :] - plane_a[maps * low + m, rows, :]
+                right_part = plane_b[maps * high + m, rows, :] - plane_b[maps * low + m, rows, :]
                 merged = jnp.where(lane >= right, left_part, right_part)
                 summed[m] += pltpu.roll(merged, LANES - right, axis=1)
+            low = high
         for m in range(maps):
             keep[j, m] = summed[m]
 
         @pl.when(b == 1)
         def _():
-            send_v[at] = keep[j].astype(jnp.bfloat16)
-            vel_copy(at).start()
+            send_v[place] = keep[j].astype(jnp.bfloat16)
+            vel_copy(place).start()
 
         @pl.when(b == 0)
         def _():
-            vel_copy(at).wait_recv()
-            keep[j] = keep[j] + recv_v[at].astype(jnp.float32)
+            vel_copy(place).wait_recv()
+            keep[j] = keep[j] + recv_v[place].astype(jnp.float32)
 
             @pl.when(a > 0)
             def _():
-                send_x[at - block] = keep[j].astype(jnp.bfloat16)
-                epoch_copy(at - block).start()
+                send_x[place - block] = keep[j].astype(jnp.bfloat16)
+                epoch_copy(place - block).start()
 
         return carry
 
@@ -272,9 +299,7 @@
             at = (a - 1) * block + j
             epoch_copy(at).wait_recv()
             total = total + recv_x[at].astype(jnp.float32)
-        phi = jnp.maximum(total[1], phi_floor)
-        likelihood[j, 0] = total[0] / jnp.sqrt(phi)
-        flux[j, 0] = total[0] / phi
+        out[j] = total
         return carry
 
     lax.fori_loop(0, block, finish, 0)
@@ -331,6 +356,8 @@
     blocks = lax.axis_size("epoch")
     block = VELS // (blocks * lax.axis_size("vel"))
     exchange = sky == GRID_X
+    last_epoch = epochs * blocks * lax.axis_size("vel") - 1
+    runs = 1 + 2 * -(-REACH * (epochs - 1) // last_epoch)
     rows_out = -(-(tile + 2 * REACH) // 16) * 16
     slots = LANES // MARGIN
     smem = pl.BlockSpec(memory_space=pltpu.SMEM)
@@ -339,12 +366,13 @@
     half = blocks * block
     far = max(1, (blocks - 1) * block)
     scratch = [
-        pltpu.VMEM((2 * epochs, rows_out, LANES), jnp.float32),
-        pltpu.VMEM((2 * epochs, rows_out, LANES), jnp.float32),
+        pltpu.VMEM((2 * (epochs + 1), rows_out, LANES), jnp.float32),
+        pltpu.VMEM((2 * (epochs + 1), rows_out, LANES), jnp.float32),
+        pltpu.SMEM((VELS, runs), jnp.int32),
         pltpu.VMEM((rows_out, tile if exchange else tile + LANES), jnp.float32),
         pltpu.VMEM((LANES, 2 * LANES), jnp.float32),
         pltpu.VMEM((slots if exchange else 1, LANES, 2 * LANES), jnp.float32),
-        pltpu.VMEM((2, 2 * LANES, 2 * LANES), jnp.bfloat16),
+        pltpu.VMEM((2, 2, 2 * LANES, 2 * LANES), jnp.bfloat16),
         pltpu.VMEM((half, 2, tile, tile), jnp.bfloat16),
         pltpu.VMEM((half, 2, tile, tile), jnp.bfloat16),
         pltpu.VMEM((far, 2, tile, tile), jnp.bfloat16),
@@ -362,7 +390,7 @@
             dma((2, groups)), dma((2, groups)),
         ]
         operands = (offsets, psf_sigma, valid, images, variances)
-        in_specs = [smem, smem, smem, vmem, vmem]
+        in_specs = [smem, smem, vmem, vmem, vmem]
     else:
         usable = valid[:, 0].astype(jnp.float32)[:, None, None]
         inverse = usable / variances[:, 0].astype(jnp.float32)
@@ -370,17 +398,21 @@
         own = jnp.stack([scaled.astype(jnp.bfloat16), inverse.astype(jnp.bfloat16)], axis=1)
         operands = (offsets, psf_sigma) + strips(own, sky, tile)
         in_specs = [smem, smem, vmem, vmem]
-    out = jax.ShapeDtypeStruct((block, 1, tile, tile), jnp.float32)
-    return pl.pallas_call(
-        functools.partial(fused_kernel, (tile, sky, blocks, block, epochs, exchange)),
-        out_shape=(out, out),
+    sums = pl.pallas_call(
+        functools.partial(fused_kernel, (tile, sky, blocks, block, epochs, runs, exchange)),
+        out_shape=jax.ShapeDtypeStruct((block, 2, tile, tile), jnp.float32),
         in_specs=in_specs,
-        out_specs=(vmem, vmem),
+        out_specs=vmem,
         scratch_shapes=scratch,
         compiler_params=pltpu.CompilerParams(
             collective_id=0, has_side_effects=True, vmem_limit_bytes=56 * 2**20
         ),
     )(*operands)
+    psi_sum = sums[:, 0]
+    phi_sum = jnp.maximum(sums[:, 1], phi_floor)
+    likelihood = psi_sum / jnp.sqrt(phi_sum)
+    flux = psi_sum / phi_sum
+    return (likelihood[:, None], flux[:, None])
 
 
 def solution(mesh):

time: 37.2 us -> 33 us (0.89)
  Pallas kernels: 32.6 us -> 29 us
  local copies, waits for them, and re-layouts: 3.75 us -> 1.33 us
  other arithmetic: 0 us -> 1.9 us
    pallas_call x1, Pallas kernels: 32.6 us -> 29 us  [on_device(): pl.pallas_call(functools.partial(fused_kernel, (tile, sky, blocks, block,...]
    unnamed x5 -> x1, local copies, waits for them, and re-layouts: 3.75 us -> 1.33 us
    div x0 -> x1, other arithmetic: none -> 1.9 us  [on_device(): flux = psi_sum / phi_sum]
where the time goes in v3:
time: 33 us; the launch traced here: 32.8 us
  Pallas kernels  29 us (88%)
  other arithmetic  1.9 us (6%)
  local copies, waits for them, and re-layouts  1.33 us (4%)
  between operations  0.64 us (2%)
    pallas_call x1, Pallas kernels, on_device(): pl.pallas_call(functools.partial(fused_kernel, (tile, sky, blocks, block,...  29 us
    div x1, other arithmetic, on_device(): flux = psi_sum / phi_sum  1.9 us
    unnamed x1, local copies, waits for them, and re-layouts  1.33 us

profile of v3, /device:TPU:0, one launch (start us, length us, event | category | flops | bytes accessed | tf_op | source)
XLA Modules:
  0.0 32.8 jit_solution(4248086284262942254)
XLA Ops:
  0.6 1.3 %copy.7.refs_2_ = s32[16,1]{1,0:T(8,128)} copy(s32[16,1]{0,1:T(1,128)} %param.7) | data formatting | bytes 128 | tf_op args[2]
  2.0 29.0 %shard_map.68 = f32[4,2,128,128]{3,2,1,0:T(8,128)} custom-call(s32[2,16,32]{2,1,0:T(8,128)} %refs_0_.1, f32[16]{0:T(128)} %refs_1_.1, s32[16,1]{1,0:T(8,128)} %copy.7.refs_2_, bf16[16,1,128,128]{3,2,1,0:T(8,128)(2,1)} %refs_3_.1, bf16[16,1,128,128]{3,2,1,0:T(8,128)(2,1)} %refs_4_.1), custom_call_target="tpu_custom_call" | custom-call | tf_op jit(solution)/shard_map/pallas_call | solution.py:401
  30.9 1.9 %slice_divide_fusion = (f32[4,1,128,128]{3,2,1,0:T(8,128)}, f32[4,1,128,128]{3,2,1,0:T(8,128)}) fusion(f32[4,2,128,128]{3,2,1,0:T(8,128)} %shard_map.68), kind=kLoop, calls=%fused_computation.2 | loop fusion | flops 196608 | bytes 1048576 | tf_op jit(solution)/shard_map/div | solution.py:414

commit v4 on v3

--- a/solution.py
+++ b/solution.py
@@ -46,11 +46,11 @@
 def fused_kernel(plan, *refs):
     tile, sky, blocks, block, epochs, runs, exchange = plan
     if exchange:
-        (offsets, sigmas, valid, images, variances, out, plane_a, plane_b, ends, row_q,
+        (offsets, motion, sigmas, valid, images, variances, psi_out, phi_out, plane_a, plane_b, ends, ends_made, ends_sem, row_q,
          own_q, side_q, bands, send_v, recv_v, send_x, recv_x, keep, sv, rv, sx, rx,
          own, building, sent_sides, came_sides, sz, rz) = refs
     else:
-        (offsets, sigmas, own, halo, out, plane_a, plane_b, ends, row_q,
+        (offsets, motion, sigmas, own, halo, psi_out, phi_out, plane_a, plane_b, ends, ends_made, ends_sem, row_q,
          own_q, side_q, bands, send_v, recv_v, send_x, recv_x, keep, sv, rv, sx, rx) = refs
     maps = 2
     slots = LANES // MARGIN
@@ -107,7 +107,7 @@
         def weigh(e, carry):
             s = lax.rem(e, slots)
             g = e // slots
-            usable = valid[pl.ds(e, 1), :].astype(jnp.float32)
+            usable = valid[e].astype(jnp.float32)
             inverse = usable / variances[e, 0].astype(jnp.float32)
             scaled = images[e, 0].astype(jnp.float32) * inverse
             to_slot = MARGIN * s
@@ -163,16 +163,20 @@
 
     first = member * epochs
 
-    def count_runs(k, carry):
-        moved = []
-        for e in range(epochs):
-            down = jnp.abs(offsets[0, k, first + e] - offsets[0, k, first])
-            moved.append(down + jnp.abs(offsets[1, k, first + e] - offsets[1, k, first]))
-        for run in range(runs - 1):
-            ends[k, run] = sum((at <= run).astype(jnp.int32) for at in moved)
-        return carry
-
-    lax.fori_loop(0, VELS, count_runs, 0)
+    at_epoch = lax.broadcasted_iota(jnp.int32, motion.shape[1:], 1)
+    moved = jnp.zeros(motion.shape[1:], jnp.int32)
+    for way in range(2):
+        start = jnp.where(at_epoch == first, motion[way], 0)
+        moved += jnp.abs(motion[way] - jnp.sum(start, axis=1, keepdims=True))
+    held_here = (at_epoch >= first) & (at_epoch < first + epochs)
+    counted = jnp.zeros(ends_made.shape, jnp.int32)
+    at_run = lax.broadcasted_iota(jnp.int32, ends_made.shape, 1)
+    for run in range(runs - 1):
+        count = jnp.sum((held_here & (moved <= run)).astype(jnp.int32), axis=1, keepdims=True)
+        counted = jnp.where(at_run == run, count, counted)
+    ends_made[...] = counted
+    ends_copy = pltpu.make_async_copy(ends_made, ends, ends_sem)
+    ends_copy.start()
     plane_a[:maps] = jnp.zeros_like(plane_a[:maps])
     plane_b[:maps] = jnp.zeros_like(plane_b[:maps])
 
@@ -252,8 +256,10 @@
 
     def stack(slot, carry):
         a = blocks - 1 - slot // (2 * block)
-        b = 1 - lax.rem(slot // block, 2)
-        j = lax.rem(slot, block)
+        turn = lax.rem(slot, 2 * block)
+        mine = ((turn > 0) & (lax.rem(turn, 2) == 0)) | (turn == 2 * block - 1)
+        b = jnp.where(mine, 0, 1)
+        j = jnp.where(turn == 2 * block - 1, block - 1, jnp.where(mine, turn // 2 - 1, (turn + 1) // 2))
         place = a * block + j
         k = (lax.rem(group + a, blocks) * 2 + lax.rem(member + b, 2)) * block + j
         lane = lax.broadcasted_iota(jnp.int32, (tile, LANES), 1)
@@ -272,34 +278,36 @@
                 summed[m] += pltpu.roll(merged, LANES - right, axis=1)
             low = high
         for m in range(maps):
-            keep[j, m] = summed[m]
+            keep[b, j, m] = summed[m]
 
         @pl.when(b == 1)
         def _():
-            send_v[place] = keep[j].astype(jnp.bfloat16)
+            send_v[place] = keep[1, j].astype(jnp.bfloat16)
             vel_copy(place).start()
 
         @pl.when(b == 0)
         def _():
             vel_copy(place).wait_recv()
-            keep[j] = keep[j] + recv_v[place].astype(jnp.float32)
+            keep[0, j] = keep[0, j] + recv_v[place].astype(jnp.float32)
 
             @pl.when(a > 0)
             def _():
-                send_x[place - block] = keep[j].astype(jnp.bfloat16)
+                send_x[place - block] = keep[0, j].astype(jnp.bfloat16)
                 epoch_copy(place - block).start()
 
         return carry
 
+    ends_copy.wait()
     lax.fori_loop(0, 2 * blocks * block, stack, 0)
 
     def finish(j, carry):
-        total = keep[j]
+        total = keep[0, j]
         for a in range(1, blocks):
             at = (a - 1) * block + j
             epoch_copy(at).wait_recv()
             total = total + recv_x[at].astype(jnp.float32)
-        out[j] = total
+        psi_out[j] = total[0]
+        phi_out[j] = total[1]
         return carry
 
     lax.fori_loop(0, block, finish, 0)
@@ -368,7 +376,9 @@
     scratch = [
         pltpu.VMEM((2 * (epochs + 1), rows_out, LANES), jnp.float32),
         pltpu.VMEM((2 * (epochs + 1), rows_out, LANES), jnp.float32),
-        pltpu.SMEM((VELS, runs), jnp.int32),
+        pltpu.SMEM((VELS, LANES), jnp.int32),
+        pltpu.VMEM((VELS, LANES), jnp.int32),
+        dma(()),
         pltpu.VMEM((rows_out, tile if exchange else tile + LANES), jnp.float32),
         pltpu.VMEM((LANES, 2 * LANES), jnp.float32),
         pltpu.VMEM((slots if exchange else 1, LANES, 2 * LANES), jnp.float32),
@@ -377,7 +387,7 @@
         pltpu.VMEM((half, 2, tile, tile), jnp.bfloat16),
         pltpu.VMEM((far, 2, tile, tile), jnp.bfloat16),
         pltpu.VMEM((far, 2, tile, tile), jnp.bfloat16),
-        pltpu.VMEM((block, 2, tile, tile), jnp.float32),
+        pltpu.VMEM((2, block, 2, tile, tile), jnp.float32),
         dma((half,)), dma((half,)), dma((far,)), dma((far,)),
     ]
     if exchange:
@@ -389,27 +399,27 @@
             pltpu.VMEM((2, groups, 2, tile, LANES), jnp.bfloat16),
             dma((2, groups)), dma((2, groups)),
         ]
-        operands = (offsets, psf_sigma, valid, images, variances)
-        in_specs = [smem, smem, vmem, vmem, vmem]
+        operands = (offsets, offsets, psf_sigma, valid.reshape(epochs), images, variances)
+        in_specs = [smem, vmem, smem, smem, vmem, vmem]
     else:
         usable = valid[:, 0].astype(jnp.float32)[:, None, None]
         inverse = usable / variances[:, 0].astype(jnp.float32)
         scaled = images[:, 0].astype(jnp.float32) * inverse
         own = jnp.stack([scaled.astype(jnp.bfloat16), inverse.astype(jnp.bfloat16)], axis=1)
-        operands = (offsets, psf_sigma) + strips(own, sky, tile)
-        in_specs = [smem, smem, vmem, vmem]
-    sums = pl.pallas_call(
+        operands = (offsets, offsets, psf_sigma) + strips(own, sky, tile)
+        in_specs = [smem, vmem, smem, vmem, vmem]
+    out = jax.ShapeDtypeStruct((block, tile, tile), jnp.float32)
+    psi_sum, phi_sum = pl.pallas_call(
         functools.partial(fused_kernel, (tile, sky, blocks, block, epochs, runs, exchange)),
-        out_shape=jax.ShapeDtypeStruct((block, 2, tile, tile), jnp.float32),
+        out_shape=(out, out),
         in_specs=in_specs,
-        out_specs=vmem,
+        out_specs=(vmem, vmem),
         scratch_shapes=scratch,
         compiler_params=pltpu.CompilerParams(
             collective_id=0, has_side_effects=True, vmem_limit_bytes=56 * 2**20
         ),
     )(*operands)
-    psi_sum = sums[:, 0]
-    phi_sum = jnp.maximum(sums[:, 1], phi_floor)
+    phi_sum = jnp.maximum(phi_sum, phi_floor)
     likelihood = psi_sum / jnp.sqrt(phi_sum)
     flux = psi_sum / phi_sum
     return (likelihood[:, None], flux[:, None])

time: 33 us -> 31.5 us (0.955)
  local copies, waits for them, and re-layouts: 1.33 us -> 0 us
    div x1 -> x0, other arithmetic: 1.9 us -> none  [on_device(): flux = psi_sum / phi_sum]
    unnamed x0 -> x1, other arithmetic: none -> 1.89 us
    unnamed x1 -> x0, local copies, waits for them, and re-layouts: 1.33 us -> none
where the time goes in v4:
time: 31.5 us; the launch traced here: 31.4 us
  Pallas kernels  28.8 us (91%)
  other arithmetic  1.89 us (6%)
  between operations  0.64 us (2%)
    pallas_call x1, Pallas kernels, on_device(): pl.pallas_call(functools.partial(fused_kernel, (tile, sky, blocks, block,...  28.8 us
    unnamed x1, other arithmetic  1.89 us

profile of v4, /device:TPU:0, one launch (start us, length us, event | category | flops | bytes accessed | tf_op | source)
XLA Modules:
  0.0 31.4 jit_solution(3457751246433836201)
XLA Ops:
  0.6 28.8 %shard_map.68 = (f32[4,128,128]{2,1,0:T(8,128)}, f32[4,128,128]{2,1,0:T(8,128)}) custom-call(s32[2,16,32]{2,1,0:T(8,128)} %refs_1_.1, s32[2,16,32]{2,1,0:T(8,128)} %refs_1_.1, f32[16]{0:T(128)} %refs_2_.1, s32[16]{0:T(128)} %bitcast.9, bf16[16,1,128,128]{3,2,1,0:T(8,128)(2,1)} %refs_4_.1, bf16[16,1,128,128]{3,2,1,0:T(8,128)(2,1)} %refs_5_.1), custom_call_target="tpu_custom_call" | custom-call | tf_op jit(solution)/shard_map/pallas_call | solution.py:412
  29.5 1.9 %divide_bitcast_fusion = (f32[4,1,128,128]{3,2,1,0:T(8,128)}, f32[4,1,128,128]{3,2,1,0:T(8,128)}) fusion(f32[4,128,128]{2,1,0:T(8,128)} %get-tuple-element.4, f32[4,128,128]{2,1,0:T(8,128)} %get-tuple-element.5), kind=kLoop, calls=%fused_computation | loop fusion | flops 196608 | bytes 1048576

commit v5 on v4

--- a/solution.py
+++ b/solution.py
@@ -44,7 +44,7 @@
 
 
 def fused_kernel(plan, *refs):
-    tile, sky, blocks, block, epochs, runs, exchange = plan
+    tile, sky, blocks, block, epochs, runs, widths, exchange = plan
     if exchange:
         (offsets, motion, sigmas, valid, images, variances, psi_out, phi_out, plane_a, plane_b, ends, ends_made, ends_sem, row_q,
          own_q, side_q, bands, send_v, recv_v, send_x, recv_x, keep, sv, rv, sx, rx,
@@ -53,7 +53,6 @@
         (offsets, motion, sigmas, own, halo, psi_out, phi_out, plane_a, plane_b, ends, ends_made, ends_sem, row_q,
          own_q, side_q, bands, send_v, recv_v, send_x, recv_x, keep, sv, rv, sx, rx) = refs
     maps = 2
-    slots = LANES // MARGIN
     rows_in = row_q.shape[1]
     rows_out = plane_a.shape[1]
     width = 2 * LANES
@@ -66,6 +65,13 @@
     after = lax.rem(me + 1, sky)
     partner = 1 - member
 
+    if exchange:
+        wide, slots = widths[0]
+        for at, (each_wide, each_slots) in enumerate(widths):
+            here = 2 * group + member == at
+            wide = jnp.where(here, each_wide, wide)
+            slots = jnp.where(here, each_slots, slots)
+
     barrier = pltpu.get_barrier_semaphore()
     greeted = 1
     pl.semaphore_signal(barrier, inc=1, device_id={"vel": partner}, device_id_type=mesh_id)
@@ -110,14 +116,14 @@
             usable = valid[e].astype(jnp.float32)
             inverse = usable / variances[e, 0].astype(jnp.float32)
             scaled = images[e, 0].astype(jnp.float32) * inverse
-            to_slot = MARGIN * s
-            to_mirror = MARGIN * (slots - 1 - s)
+            to_slot = wide * s
+            to_mirror = wide * (slots - 1 - s)
             for m, field in enumerate((scaled, inverse)):
                 own[e, m] = field.astype(jnp.bfloat16)
                 low = pltpu.roll(field, to_mirror, axis=1)
-                high = pltpu.roll(field, to_slot + MARGIN, axis=1)
-                at_low = (lane >= to_mirror) & (lane < to_mirror + MARGIN)
-                at_high = (lane >= to_slot) & (lane < to_slot + MARGIN)
+                high = pltpu.roll(field, lax.rem(to_slot + wide, LANES), axis=1)
+                at_low = (lane >= to_mirror) & (lane < to_mirror + wide)
+                at_high = (lane >= to_slot) & (lane < to_slot + wide)
                 building[0, m] = jnp.where(at_low, low, building[0, m])
                 building[1, m] = jnp.where(at_high, high, building[1, m])
 
@@ -150,14 +156,18 @@
     shifted_out = lax.broadcasted_iota(jnp.int32, shape, 1) - REACH
     own_q[...] = exponents(held - shifted_out)
     if exchange:
-        for s in range(slots):
-            low, high = MARGIN * s, MARGIN * (slots - 1 - s)
+
+        def place_strips(s, carry):
+            low, high = wide * s, wide * (slots - 1 - s)
             pixel = jnp.where(
-                (held >= low) & (held < low + MARGIN),
-                held - low - MARGIN,
-                jnp.where((held >= high) & (held < high + MARGIN), held - high + tile, 4 * tile),
+                (held >= low) & (held < low + wide),
+                held - low - wide,
+                jnp.where((held >= high) & (held < high + wide), held - high + tile, 4 * tile),
             )
             side_q[s] = exponents(pixel - shifted_out)
+            return carry
+
+        lax.fori_loop(0, slots, place_strips, 0)
     else:
         side_q[0] = exponents(positions(held + tile, tile) - shifted_out)
 
@@ -200,7 +210,7 @@
         if exchange:
             g = e // slots
             lane = lax.broadcasted_iota(jnp.int32, (tile, LANES), 1)
-            in_slot = (lane >= MARGIN * s) & (lane < MARGIN * s + MARGIN)
+            in_slot = (lane >= wide * s) & (lane < wide * s + wide)
         for m in range(maps):
             if exchange:
                 side = jnp.where(
@@ -219,7 +229,7 @@
             plane_a[at + maps] = plane_a[at] + done[:, :LANES]
             plane_b[at + maps] = plane_b[at] + done[:, LANES:]
 
-    step = 2 if epochs % 2 == 0 and slots % 2 == 0 else 1
+    step = 2 if epochs % 2 == 0 else 1
 
     def several(i, carry):
         for turn in range(step):
@@ -229,15 +239,17 @@
     if exchange:
         for g in range(groups):
 
-            @pl.when(column < GRID_X - 1)
+            @pl.when((column < GRID_X - 1) & (g * slots < epochs))
             def _():
                 side_copy(0, g).wait_recv()
 
-            @pl.when(column > 0)
+            @pl.when((column > 0) & (g * slots < epochs))
             def _():
                 side_copy(1, g).wait_recv()
 
-            lax.fori_loop(g * slots // step, min((g + 1) * slots, epochs) // step, several, 0)
+            begin = jnp.minimum(g * slots, epochs) // step
+            end = jnp.minimum((g + 1) * slots, epochs) // step
+            lax.fori_loop(begin, end, several, 0)
     else:
         lax.fori_loop(0, epochs // step, several, 0)
 
@@ -326,11 +338,11 @@
     if exchange:
 
         def drain_z(g, carry):
-            @pl.when(column > 0)
+            @pl.when((column > 0) & (g * slots < epochs))
             def _():
                 side_copy(0, g).wait_send()
 
-            @pl.when(column < GRID_X - 1)
+            @pl.when((column < GRID_X - 1) & (g * slots < epochs))
             def _():
                 side_copy(1, g).wait_send()
 
@@ -367,7 +379,10 @@
     last_epoch = epochs * blocks * lax.axis_size("vel") - 1
     runs = 1 + 2 * -(-REACH * (epochs - 1) // last_epoch)
     rows_out = -(-(tile + 2 * REACH) // 16) * 16
-    slots = LANES // MARGIN
+    devices = blocks * lax.axis_size("vel")
+    reaches = [PSFR + -(-REACH * ((at + 1) * epochs - 1) // last_epoch) for at in range(devices)]
+    widths = [(wide, LANES // wide // 2 * 2) for wide in reaches]
+    slots = max(each for _, each in widths)
     smem = pl.BlockSpec(memory_space=pltpu.SMEM)
     vmem = pl.BlockSpec(memory_space=pltpu.VMEM)
     dma = pltpu.SemaphoreType.DMA
@@ -391,7 +406,7 @@
         dma((half,)), dma((half,)), dma((far,)), dma((far,)),
     ]
     if exchange:
-        groups = -(-epochs // slots)
+        groups = -(-epochs // min(each for _, each in widths))
         scratch += [
             pltpu.VMEM((epochs, 2, tile, tile), jnp.bfloat16),
             pltpu.VMEM((2, 2, tile, LANES), jnp.float32),
@@ -410,7 +425,7 @@
         in_specs = [smem, vmem, smem, vmem, vmem]
     out = jax.ShapeDtypeStruct((block, tile, tile), jnp.float32)
     psi_sum, phi_sum = pl.pallas_call(
-        functools.partial(fused_kernel, (tile, sky, blocks, block, epochs, runs, exchange)),
+        functools.partial(fused_kernel, (tile, sky, blocks, block, epochs, runs, widths, exchange)),
         out_shape=(out, out),
         in_specs=in_specs,
         out_specs=(vmem, vmem),

time: 31.5 us -> 30.8 us (0.978)
  Pallas kernels: 28.8 us -> 28.1 us
    pallas_call x1, Pallas kernels: 28.8 us -> 28.1 us  [on_device(): pl.pallas_call(functools.partial(fused_kernel, (tile, sky, blocks, block,...]
where the time goes in v5:
time: 30.8 us; the launch traced here: 30.7 us
  Pallas kernels  28.1 us (91%)
  other arithmetic  1.89 us (6%)
  between operations  0.64 us (2%)
    pallas_call x1, Pallas kernels, on_device(): pl.pallas_call(functools.partial(fused_kernel, (tile, sky, blocks, block,...  28.1 us
    unnamed x1, other arithmetic  1.89 us

profile of v5, /device:TPU:0, one launch (start us, length us, event | category | flops | bytes accessed | tf_op | source)
XLA Modules:
  0.0 30.7 jit_solution(16817976237050711196)
XLA Ops:
  0.6 28.1 %shard_map.68 = (f32[4,128,128]{2,1,0:T(8,128)}, f32[4,128,128]{2,1,0:T(8,128)}) custom-call(s32[2,16,32]{2,1,0:T(8,128)} %refs_1_.1, s32[2,16,32]{2,1,0:T(8,128)} %refs_1_.1, f32[16]{0:T(128)} %refs_2_.1, s32[16]{0:T(128)} %bitcast.9, bf16[16,1,128,128]{3,2,1,0:T(8,128)(2,1)} %refs_4_.1, bf16[16,1,128,128]{3,2,1,0:T(8,128)(2,1)} %refs_5_.1), custom_call_target="tpu_custom_call" | custom-call | tf_op jit(solution)/shard_map/pallas_call | solution.py:427
  28.8 1.9 %divide_bitcast_fusion = (f32[4,1,128,128]{3,2,1,0:T(8,128)}, f32[4,1,128,128]{3,2,1,0:T(8,128)}) fusion(f32[4,128,128]{2,1,0:T(8,128)} %get-tuple-element.4, f32[4,128,128]{2,1,0:T(8,128)} %get-tuple-element.5), kind=kLoop, calls=%fused_computation | loop fusion | flops 196608 | bytes 1048576

commit v6 on v5

--- a/solution.py
+++ b/solution.py
@@ -431,7 +431,7 @@
         out_specs=(vmem, vmem),
         scratch_shapes=scratch,
         compiler_params=pltpu.CompilerParams(
-            collective_id=0, has_side_effects=True, vmem_limit_bytes=56 * 2**20
+            collective_id=0, has_side_effects=True, vmem_limit_bytes=28 * 2**20
         ),
     )(*operands)
     phi_sum = jnp.maximum(phi_sum, phi_floor)

time: 30.8 us -> 32.2 us (1.045)
  local copies, waits for them, and re-layouts: 0 us -> 3.45 us
  Pallas kernels: 28.1 us -> 26.9 us
  other arithmetic: 1.89 us -> 0.87 us
    unnamed x0 -> x10, local copies, waits for them, and re-layouts: none -> 3.45 us
    pallas_call x1, Pallas kernels: 28.1 us -> 26.9 us  [on_device(): pl.pallas_call(functools.partial(fused_kernel, (tile, sky, blocks, block,...]
    unnamed x1, other arithmetic: 1.89 us -> 0.87 us
where the time goes in v6:
time: 32.2 us; the launch traced here: 31.9 us
  Pallas kernels  26.9 us (84%)
  local copies, waits for them, and re-layouts  3.45 us (11%)
  other arithmetic  0.87 us (3%)
  between operations  0.66 us (2%)
    pallas_call x1, Pallas kernels, on_device(): pl.pallas_call(functools.partial(fused_kernel, (tile, sky, blocks, block,...  26.9 us
    unnamed x10, local copies, waits for them, and re-layouts  3.45 us
    unnamed x1, other arithmetic  0.87 us

profile of v6, /device:TPU:0, one launch (start us, length us, event | category | flops | bytes accessed | tf_op | source)
XLA Modules:
  0.0 31.9 jit_solution(376978438423210388)
XLA Ops:
  0.6 0.0 copy-start.3
  0.6 0.0 copy-start.4
  0.7 0.6 %copy-done.3 = f32[16]{0:T(128)S(1)} copy-done((f32[16]{0:T(128)S(1)}, f32[16]{0:T(128)}, u32[]{:S(2)}) %copy-start.3) | copy-done | bytes 88
  1.3 0.0 copy-done.4
  1.3 0.0 copy-start
  1.3 1.0 %copy-done = bf16[16,1,128,128]{3,2,1,0:T(8,128)(2,1)S(1)} copy-done((bf16[16,1,128,128]{3,2,1,0:T(8,128)(2,1)S(1)}, bf16[16,1,128,128]{3,2,1,0:T(8,128)(2,1)}, u32[]{:S(2)}) %copy-start) | copy-done | bytes 524312
  2.3 0.0 copy-start.1
  2.3 1.0 %copy-done.1 = bf16[16,1,128,128]{3,2,1,0:T(8,128)(2,1)S(1)} copy-done((bf16[16,1,128,128]{3,2,1,0:T(8,128)(2,1)S(1)}, bf16[16,1,128,128]{3,2,1,0:T(8,128)(2,1)}, u32[]{:S(2)}) %copy-start.1) | copy-done | bytes 524312
  3.4 0.0 copy-start.2
  3.4 0.7 %copy-done.2 = s32[2,16,32]{2,1,0:T(8,128)S(1)} copy-done((s32[2,16,32]{2,1,0:T(8,128)S(1)}, s32[2,16,32]{2,1,0:T(8,128)}, u32[]{:S(2)}) %copy-start.2) | copy-done | bytes 4120
  4.1 26.9 %shard_map.68 = (f32[4,128,128]{2,1,0:T(8,128)S(1)}, f32[4,128,128]{2,1,0:T(8,128)S(1)}) custom-call(s32[2,16,32]{2,1,0:T(8,128)S(1)} %copy-done.2, s32[2,16,32]{2,1,0:T(8,128)S(1)} %copy-done.2, f32[16]{0:T(128)S(1)} %copy-done.3, s32[16]{0:T(128)S(1)} %bitcast.9, bf16[16,1,128,128]{3,2,1,0:T(8,128)(2,1)S(1)} %copy-done, bf16[16,1,128,128]{3,2,1,0:T(8,128)(2,1)S(1)} %copy-done.1), custom_call_target="tpu_custom_call" | custom-call | tf_op jit(solution)/shard_map/pallas_call | solution.py:427
  31.0 0.9 %divide_bitcast_fusion = (f32[4,1,128,128]{3,2,1,0:T(8,128)}, f32[4,1,128,128]{3,2,1,0:T(8,128)}) fusion(f32[4,128,128]{2,1,0:T(8,128)S(1)} %get-tuple-element.4, f32[4,128,128]{2,1,0:T(8,128)S(1)} %get-tuple-element.5), kind=kLoop, calls=%fused_computation | loop fusion | flops 196608 | bytes 1048576
Async XLA Ops:
  0.6 0.7 %copy-start.3 = (f32[16]{0:T(128)S(1)}, f32[16]{0:T(128)}, u32[]{:S(2)}) copy-start(f32[16]{0:T(128)} %refs_2_.1) | copy-start | bytes 196
  0.6 0.7 %copy-start.4 = (s32[16,1]{0,1:T(1,128)S(1)}, s32[16,1]{0,1:T(1,128)}, u32[]{:S(2)}) copy-start(s32[16,1]{0,1:T(1,128)} %param.7) | copy-start | bytes 196
  1.3 1.0 %copy-start = (bf16[16,1,128,128]{3,2,1,0:T(8,128)(2,1)S(1)}, bf16[16,1,128,128]{3,2,1,0:T(8,128)(2,1)}, u32[]{:S(2)}) copy-start(bf16[16,1,128,128]{3,2,1,0:T(8,128)(2,1)} %refs_4_.1) | copy-start | bytes 1572868
  2.3 1.0 %copy-start.1 = (bf16[16,1,128,128]{3,2,1,0:T(8,128)(2,1)S(1)}, bf16[16,1,128,128]{3,2,1,0:T(8,128)(2,1)}, u32[]{:S(2)}) copy-start(bf16[16,1,128,128]{3,2,1,0:T(8,128)(2,1)} %refs_5_.1) | copy-start | bytes 1572868
  3.4 0.7 %copy-start.2 = (s32[2,16,32]{2,1,0:T(8,128)S(1)}, s32[2,16,32]{2,1,0:T(8,128)}, u32[]{:S(2)}) copy-start(s32[2,16,32]{2,1,0:T(8,128)} %refs_1_.1) | copy-start | bytes 12292
